TPU v7x, 32 devices: a whole 2x2x4 slice. The times are simulated.
32 devices in a mesh: face: 2 (over x), gx: 4 (over y, core), gy: 4 (over z).
Axes of the slice: x: 2, y: 2, z: 4, core: 2. Of those that a mesh axis runs over, the one named last changes fastest.
Arguments:
- atmos_state: float32 [4, 32, 256, 512], P(None, None, ('face', 'gy'), 'gx'), may hold values from -5 to 5
- atmos_kappa: float32 [256, 512], P(('face', 'gy'), 'gx'), may hold values from 0.05 to 0.24
- ocean_tracers: float32 [2, 32, 256, 512], P(None, None, ('face', 'gy'), 'gx'), may hold values from -5 to 5
- ocean_flow: float32 [2, 32, 256, 512], P(None, None, ('face', 'gy'), 'gx'), may hold values from -0.3 to 0.3
- ocean_kappa: float32 [32, 256, 512], P(None, ('face', 'gy'), 'gx'), may hold values from 0.02 to 0.08
- sea_mask: int32 [256, 512], P(('face', 'gy'), 'gx'), may hold values 0 or 1
- xgrid_atmos_cell: int32 [24, 12, 1024], P(('face', 'gy'), 'gx'), may hold values from 0 to 4095
- xgrid_ocean_cell: int32 [24, 12, 1024], P(('face', 'gy'), 'gx'), may hold values from 0 to 4095
- xgrid_weights: float32 [2, 24, 12, 1024], P(None, ('face', 'gy'), 'gx'), may hold values from 0 to 0.6, as said below
Outputs:
- atmos_next: float32 [4, 32, 256, 512], P(None, None, ('face', 'gy'), 'gx')
- ocean_next: float32 [2, 32, 256, 512], P(None, None, ('face', 'gy'), 'gx')
- ocean_stress: float32 [2, 256, 512], P(None, ('face', 'gy'), 'gx')
Inputs may be any that keep to these rules, and one draw needn't show every extreme that they name: `xgrid_weights`: both weights of a slot are zero exactly where the slot carries no intersection and positive elsewhere; within each aligned block of 1024 slots the live ones come first; the run of a block's own offset (a = b = 1) is full, and runs pointing below the first or above the last row of blocks are empty.
All inputs are finite; a program needn't handle non-finite values. No bound on the sum of `sea_mask` on one device may be relied on, other than what follows from the above.
Results may differ from a plain program's by a relative error of at most 0.00002.
Values sent between devices are 32-bit elements; how exact they have to be, the bound alone decides.
A program may use at most 192 MiB of HBM per device.

v0:
```python
import jax
import jax.numpy as jnp
from jax import lax
from jax.sharding import PartitionSpec as P

ITERS = 24
ATM_SUB = 4


current_scale = 2.0
atmos_gain = 0.5
ocean_gain = 0.02


def partner_2(value, axis, distance):
    mask = 2**distance
    pairs = [(source, source ^ mask) for source in range(lax.axis_size(axis))]
    return lax.ppermute(value, axis, pairs)


def padded_2(block, sides, width):
    for axis, dim in sides:
        count = lax.axis_size(axis)
        forward = [(i, i + 1) for i in range(count - 1)]
        forward.append((count - 1, 0))
        backward = [(target, source) for source, target in forward]
        low = lax.ppermute(
            lax.slice_in_dim(block, block.shape[dim] - width, None, axis=dim), axis, forward
        )
        high = lax.ppermute(lax.slice_in_dim(block, 0, width, axis=dim), axis, backward)
        block = jnp.concatenate([low, block, high], axis=dim)
    return block


def bulk_fluxes(air_vals, sea_vals):
    temp_air, humid_air, wind_east, wind_north = (
        air_vals[0],
        air_vals[1],
        air_vals[2],
        air_vals[3],
    )
    sea_temp, current_east, current_north = (sea_vals[0], sea_vals[1], sea_vals[2])
    shear_east = wind_east - current_east
    shear_north = wind_north - current_north
    wind_speed = jnp.sqrt(shear_east * shear_east + shear_north * shear_north + 0.25)
    richardson = (temp_air - sea_temp) / (wind_speed * wind_speed)
    heat_coeff = 0.1 + 0.4 * jax.nn.sigmoid(-2.0 * richardson)
    drag_coeff = 0.2 + 0.1 * jnp.tanh(wind_speed)
    sensible = heat_coeff * wind_speed * (sea_temp - temp_air)
    latent = heat_coeff * wind_speed * (0.5 * jnp.exp(0.3 * sea_temp) - humid_air)
    return jnp.stack(
        [
            sensible,
            latent,
            drag_coeff * wind_speed * shear_east,
            drag_coeff * wind_speed * shear_north,
        ]
    )


def tendency(
    tracers,
    west_cells,
    east_cells,
    south_cells,
    north_cells,
    east_flow,
    north_flow,
    diffusion,
    forcing,
):
    change = -jnp.maximum(east_flow, 0.0) * (tracers - west_cells) + jnp.maximum(
        -east_flow, 0.0
    ) * (east_cells - tracers)
    change = (
        change
        - jnp.maximum(north_flow, 0.0) * (tracers - south_cells)
        + jnp.maximum(-north_flow, 0.0) * (north_cells - tracers)
    )
    change = change + diffusion * (
        west_cells + east_cells + south_cells + north_cells - 4.0 * tracers
    )
    return change.at[:, 0].add(forcing)


def mirrored(top_rows):
    for bit_index in range(lax.axis_size("gx").bit_length() - 1):
        top_rows = partner_2(top_rows, "gx", bit_index)
    return top_rows


def extend(field, depth, fold_signs, south_signs):
    rows = field.shape[2]
    padded = padded_2(field, ((("face", "gy"), 2), ("gx", 3)), depth)
    partner = mirrored(padded[:, :, rows : rows + depth, :])[:, :, ::-1, ::-1] * fold_signs
    bottom = padded[:, :, depth : 2 * depth, :][:, :, ::-1, :] * south_signs
    position = lax.axis_index(("face", "gy"))
    south_part = jnp.where(position == 0, bottom, padded[:, :, :depth])
    north_part = jnp.where(
        position == lax.axis_size(("face", "gy")) - 1, partner, padded[:, :, rows + depth :]
    )
    return jnp.concatenate([south_part, padded[:, :, depth : rows + depth], north_part], axis=2)


def local(
    atmos_state,
    atmos_kappa,
    ocean_tracers,
    ocean_flow,
    ocean_kappa,
    sea_mask,
    xgrid_atmos_cell,
    xgrid_ocean_cell,
    xgrid_weights,
):
    rows_atmos, cols_atmos = (atmos_state.shape[2], atmos_state.shape[3])
    rows_ocean, cols_ocean = (ocean_tracers.shape[2], ocean_tracers.shape[3])
    levels_ocean = ocean_tracers.shape[1]
    slot_count = xgrid_atmos_cell.shape[2]
    atmos_cells = rows_atmos * cols_atmos
    ocean_cells = rows_ocean * cols_ocean
    lowest = atmos_state[:, 0].reshape(4, atmos_cells)
    surface = jnp.stack(
        [ocean_tracers[0, 0], current_scale * ocean_flow[0, 0], current_scale * ocean_flow[1, 0]]
    ).reshape(3, ocean_cells)
    atmos_slots = xgrid_atmos_cell.reshape(-1)
    air_vals = jnp.take(lowest, atmos_slots, axis=1)
    nearby = padded_2(surface[:, None, None, :], ((("face", "gy"), 1), ("gx", 2)), 1).reshape(3, -1)
    offsets = lax.broadcasted_iota(jnp.int32, (3, 3, slot_count), 0) * 3 + lax.broadcasted_iota(
        jnp.int32, (3, 3, slot_count), 1
    )
    places = (offsets * ocean_cells + xgrid_ocean_cell).reshape(-1)
    sea_vals = jnp.take(nearby, places, axis=1)
    fluxes = bulk_fluxes(air_vals, sea_vals)
    blocks = (
        jnp.zeros((4, 9 * ocean_cells), jnp.float32)
        .at[:, places]
        .add(xgrid_weights[1].reshape(-1) * fluxes)
    )
    blocks = blocks.reshape(4, 3, 3, ocean_cells)
    returned = padded_2(blocks, ((("face", "gy"), 1), ("gx", 2)), 1)[:, 0::2, 0::2]
    ocean_flux = jnp.sum(returned, axis=(1, 2))
    atmos_flux = (
        jnp.zeros((4, atmos_cells), jnp.float32)
        .at[:, atmos_slots]
        .add(xgrid_weights[0].reshape(-1) * fluxes)
    )
    atmos_flux = atmos_flux.reshape(4, rows_atmos, cols_atmos)
    flux_gains = jnp.array([atmos_gain, atmos_gain, -atmos_gain, -atmos_gain], jnp.float32)
    atmos_now = atmos_state.at[:, 0].add(flux_gains[:, None, None] * atmos_flux)
    for _ in range(ATM_SUB):
        above_cells = jnp.concatenate([atmos_now[:, 1:], atmos_now[:, -1:]], axis=1)
        below_cells = jnp.concatenate([atmos_now[:, :1], atmos_now[:, :-1]], axis=1)
        atmos_now = atmos_now + atmos_kappa * (above_cells + below_cells - 2.0 * atmos_now)
    ocean_flux = ocean_flux.reshape(4, rows_ocean, cols_ocean)
    sea_weight = sea_mask.astype(jnp.float32)
    forcing_slab = jnp.zeros((levels_ocean, rows_ocean, cols_ocean), jnp.float32)
    forcing_slab = forcing_slab.at[0].set(-ocean_gain * (ocean_flux[0] + ocean_flux[1]))
    forcing_slab = forcing_slab.at[1].set(ocean_gain * ocean_flux[1])
    mask_levels = jnp.broadcast_to(sea_weight[None], (levels_ocean, rows_ocean, cols_ocean))
    statics = jnp.stack([ocean_flow[0], ocean_flow[1], ocean_kappa, mask_levels, forcing_slab])
    depth = 4
    tracer_signs = jnp.ones((2, 1, 1, 1), jnp.float32)
    fold_signs = jnp.array([-1.0, -1.0, 1.0, 1.0, 1.0], jnp.float32).reshape(5, 1, 1, 1)
    south_signs = jnp.array([1.0, -1.0, 1.0, 1.0, 1.0], jnp.float32).reshape(5, 1, 1, 1)
    widened = extend(statics, depth, fold_signs, south_signs)

    def advance(iteration, tracers):
        grown = extend(tracers, depth, tracer_signs, tracer_signs)
        for inner in range(depth):
            margin = inner + 1
            near = widened[
                :, :, margin : widened.shape[2] - margin, margin : widened.shape[3] - margin
            ]
            center = grown[:, :, 1:-1, 1:-1]
            near_forcing = jnp.stack([near[4, 0], near[4, 1]])
            change = tendency(
                center,
                grown[:, :, 1:-1, :-2],
                grown[:, :, 1:-1, 2:],
                grown[:, :, :-2, 1:-1],
                grown[:, :, 2:, 1:-1],
                near[0],
                near[1],
                near[2],
                near_forcing,
            )
            grown = center + near[3] * change
        return grown

    ocean_now = lax.fori_loop(0, ITERS // depth, advance, ocean_tracers)
    ocean_stress = sea_weight * ocean_flux[2:4]
    return (atmos_now, ocean_now, ocean_stress)


def solution(mesh):
    placed = (
        P(None, None, ("face", "gy"), "gx"),
        P(("face", "gy"), "gx"),
        P(None, None, ("face", "gy"), "gx"),
        P(None, None, ("face", "gy"), "gx"),
        P(None, ("face", "gy"), "gx"),
        P(("face", "gy"), "gx"),
        P(("face", "gy"), "gx", None),
        P(("face", "gy"), "gx", None),
        P(None, ("face", "gy"), "gx", None),
    )
    return jax.shard_map(
        local,
        mesh=mesh,
        in_specs=placed,
        out_specs=(
            P(None, None, ("face", "gy"), "gx"),
            P(None, None, ("face", "gy"), "gx"),
            P(None, ("face", "gy"), "gx"),
        ),
        check_vma=False,
    )
```

profile of v0, /device:TPU:24, one launch (start us, length us, event | category | flops | bytes accessed | tf_op | source)
XLA Modules:
  0.0 978.7 jit_solution(11361925396555179367)
XLA Ops:
  9.5 32.5 %gather_fusion = f32[9216,4]{1,0:T(8,128)} fusion(f32[4,4096]{0,1:T(8,128)} %bitcast.134, s32[9216]{0:T(1024)S(1)} %broadcast_clamp_fusion.1), kind=kCustom, calls=%fused_computation | custom fusion | bytes 331776 | tf_op jit(solution)/shard_map/jit(_take)/gather | solution.py:127
  55.1 9.5 copy.216
  64.6 37.3 %gather_fusion.1 = f32[9216,3]{1,0:T(8,128)} fusion(f32[3,36864]{0,1:T(8,128)} %bitcast.131, s32[9216]{0:T(1024)S(1)} %copy-done.46), kind=kCustom, calls=%fused_computation.1 | custom fusion | bytes 258048 | tf_op jit(solution)/shard_map/jit(_take)/gather | solution.py:133
  108.9 51.3 %scatter_custom_fusion = f32[4,4096]{0,1:T(8,128)} fusion(s32[9216]{0:T(1024)} %bitcast.153, f32[9216,4]{1,0:T(8,128)} %copy.218, f32[]{:T(128)} %constant.298.clone.1), kind=kCustom, calls=%fused_computation.83 | custom fusion | flops 36864 | bytes 66048 | tf_op jit(solution)/shard_map/scatter-add | solution.py:146
  169.6 57.2 %scatter_custom_fusion.1 = f32[4,36864]{0,1:T(8,128)} fusion(s32[9216]{0:T(1024)} %bitcast.151, f32[9216,4]{1,0:T(8,128)} %copy.220, f32[]{:T(128)} %constant.298.clone.1), kind=kCustom, calls=%fused_computation.55 | custom fusion | flops 36864 | bytes 590336 | tf_op jit(solution)/shard_map/scatter-add | solution.py:138
  226.8 10.5 %copy.221 = f32[4,3,3,4096]{3,0,2,1:T(4,128)S(1)} copy(f32[4,3,3,4096]{0,3,2,1:T(8,128)} %bitcast.130) | data formatting | bytes 1179648 | tf_op jit(solution)/shard_map/reshape | solution.py:140
  246.5 4.9 collective-permute-done.11
  275.0 9.8 %copy.228 = f32[5,32,32,128]{2,1,3,0:T(8,128)} copy(f32[5,32,32,128]{3,2,1,0:T(8,128)} %copy-done.33) | data formatting | bytes 5242880 | tf_op jit(solution)/shard_map/stack | solution.py:161
  288.5 6.6 copy.227
  295.1 6.6 copy.229
  312.7 12.9 %pad_maximum_fusion.5 = f32[5,32,40,136]{2,1,3,0:T(8,128)S(1)} fusion(f32[5,32,40,4]{2,1,3,0:T(8,128)S(1)} %collective-permute-done.17, f32[5,32,4,128]{2,1,3,0:T(8,128)} %copy.229, f32[5,32,32,128]{2,1,3,0:T(8,128)} %copy.228, f32[5,32,4,128]{2,1,3,0:T(8,128)} %copy.227, f32[5,32,40,4]{2,1,3,0:T(8,128)S(1)} %collective-permute-done.16), kind=kLoop, calls=%fused_computation.53 | loop fusion | flops 3481600 | bytes 6963200 | tf_op jit(solution)/shard_map/concatenate | solution.py:31
  325.6 10.7 %fusion.25 = (f32[5,32,4,136]{2,1,3,0:T(8,128)}, f32[5,32,4,136]{2,1,3,0:T(8,128)}) fusion(f32[5,32,40,136]{2,1,3,0:T(8,128)S(1)} %pad_maximum_fusion.5), kind=kLoop, calls=%fused_computation.143 | loop fusion | bytes 1392640 | tf_op jit(solution)/shard_map/slice | solution.py:96
  336.3 8.2 copy.230
  353.1 11.2 %slice.823 = f32[5,32,32,136]{2,1,3,0:T(8,128)} slice(f32[5,32,40,136]{2,1,3,0:T(8,128)} %copy-done.2), slice={[0:5], [0:32], [4:36], [0:136]} | slice | bytes 5570560 | tf_op jit(solution)/shard_map/slice | solution.py:102
  364.3 18.0 %rev.18 = f32[5,32,4,136]{2,1,3,0:T(8,128)} reverse(f32[5,32,4,136]{2,1,3,0:T(8,128)} %get-tuple-element.383), dimensions={2} | reverse | bytes 696320 | tf_op jit(solution)/shard_map/rev | solution.py:96
  382.3 11.6 %copy.246 = f32[5,32,32,136]{3,2,1,0:T(8,128)} copy(f32[5,32,32,136]{2,1,3,0:T(8,128)} %slice.823) | data formatting | bytes 5570560 | tf_op jit(solution)/shard_map/while | solution.py:191
  393.9 6.1 copy.231
  399.9 18.2 %rev.19 = f32[5,32,4,136]{2,1,3,0:T(8,128)} reverse(f32[5,32,4,136]{2,1,3,0:T(8,128)} %copy.231), dimensions={2,3} | reverse | bytes 696320 | tf_op jit(solution)/shard_map/rev | solution.py:95
  418.1 24.6 %slice_select_fusion.1 = (f32[5,32,4,136]{2,1,3,0:T(8,128)}, f32[5,32,4,136]{2,1,3,0:T(8,128)}) fusion(f32[5,32,40,136]{2,1,3,0:T(8,128)} %copy-done.2, f32[5,32,4,136]{2,1,3,0:T(8,128)} %rev.18, f32[5]{0:T(128)S(1)} %copy-done.54, pred[]{:T(512)S(6)} %eq.18, f32[5,32,4,136]{2,1,3,0:T(8,128)} %rev.19, f32[5]{0:T(128)S(1)} %copy-done.53, pred[]{:T(512)S(6)} %eq.19), kind=kLoop, calls=%fused_computation.52 | loop fusion | flops 348160 | bytes 2089002 | tf_op jit(solution)/shard_map/jit(_where)/select_n | solution.py:98
  442.8 10.4 %pad_maximum_fusion.6 = f32[5,32,40,136]{2,1,3,0:T(8,128)S(1)} fusion(f32[5,32,4,136]{2,1,3,0:T(8,128)} %get-tuple-element.382, f32[5,32,32,136]{2,1,3,0:T(8,128)S(1)} %bitcast.129, f32[5,32,4,136]{2,1,3,0:T(8,128)} %get-tuple-element.381), kind=kLoop, calls=%fused_computation.54 | loop fusion | flops 1740800 | bytes 6963200 | tf_op jit(solution)/shard_map/concatenate | solution.py:102
  457.6 11.8 %copy.236 = f32[5,32,40,136]{3,2,1,0:T(8,128)} copy(f32[5,32,40,136]{2,1,3,0:T(8,128)} %copy-done.22) | data formatting | bytes 6963200 | tf_op jit(solution)/shard_map/while | solution.py:191
  469.4 4.8 slice_negate_fusion
  474.2 5.5 slice_negate_fusion.2
  479.7 5.5 slice_negate_fusion.4
  504.8 472.5 %while.19 = (s32[]{:T(128)}, f32[2,32,32,128]{3,2,0,1:T(8,128)S(1)}, f32[5,32,40,136]{3,2,1,0:T(8,128)}, f32[1,32,38,134]{3,2,1,0:T(8,128)}, f32[1,32,38,134]{3,...) while((s32[]{:T(128)}, ...), condition=%wide.region_4.5_spmd, body=%wide.region_3.4_spmd.sunk | while | flops 29846140 | bytes 181502032 | solution.py:191
  509.8 6.4 slice_bitcast_fusion.19
  583.7 4.7 collective-permute-start.1
  588.4 6.4 slice_bitcast_fusion.19
  667.3 6.4 slice_bitcast_fusion.19
  745.9 6.4 slice_bitcast_fusion.19
  824.7 6.4 slice_bitcast_fusion.19
  903.3 6.4 slice_bitcast_fusion.19
  (801 shorter events, 545.5 us)
Async XLA Ops:
  3.9 43.8 %collective-permute-start.6 = (f32[3,1,1,4096]{3,2,1,0:T(1,128)}, f32[3,1,1,4096]{3,2,1,0:T(1,128)S(1)}, u32[]{:S(2)}, u32[]{:S(2)}) collective-permute-start(f32[3,1,1,4096]{3,2,1,0:T(1,128)} %pad_maximum_fusion.21), channel_id=1, source_target_pairs={{0,1},{1,2},{2,3},{3,16},{16,17},{17,18},{18,19},{19,0},{4,5},{5,6... | collective-permute-start | bytes 147464 | tf_op jit(solution)/shard_map/ppermute | solution.py:27
  5.0 42.6 %collective-permute-start.7 = (f32[3,1,1,4096]{3,2,1,0:T(1,128)}, f32[3,1,1,4096]{3,2,1,0:T(1,128)}, u32[]{:S(2)}, u32[]{:S(2)}) collective-permute-start(f32[3,1,1,4096]{3,2,1,0:T(1,128)} %pad_maximum_fusion.21), channel_id=1, source_target_pairs={{1,0},{2,1},{3,2},{16,3},{17,16},{18,17},{19,18},{0,19},{5,4},{6,5... | collective-permute-start | bytes 147464 | tf_op jit(solution)/shard_map/ppermute | solution.py:30
  237.3 9.2 collective-permute-start.10
  241.2 10.2 %collective-permute-start.11 = (f32[4,1,3,4096]{3,0,2,1:T(4,128)S(1)}, f32[4,1,3,4096]{3,0,2,1:T(4,128)S(1)}, u32[]{:S(2)}, u32[]{:S(2)}) collective-permute-start(f32[4,1,3,4096]{3,0,2,1:T(4,128)S(1)} %get-tuple-element.408), channel_id=1, source_target_pairs={{1,0},{2,1},{3,2},{16,3},{17,16},{18,17},{19,18},{0,19},{5,4},{6,5... | collective-permute-start | bytes 589832 | tf_op jit(solution)/shard_map/ppermute | solution.py:30
  251.7 8.4 collective-permute-start.12
  251.7 8.9 collective-permute-start.13
  270.7 17.8 %collective-permute-start.14 = (f32[5,32,4,128]{3,1,2,0:T(8,128)S(1)}, f32[5,32,4,128]{3,1,2,0:T(8,128)}, u32[]{:S(2)}, u32[]{:S(2)}) collective-permute-start(f32[5,32,4,128]{3,1,2,0:T(8,128)S(1)} %copy.252), channel_id=1, source_target_pairs={{0,1},{1,2},{2,3},{3,16},{16,17},{17,18},{18,19},{19,0},{4,5},{5,6... | collective-permute-start | bytes 983048 | tf_op jit(solution)/shard_map/ppermute | solution.py:27
  272.6 22.5 %collective-permute-start.15 = (f32[5,32,4,128]{3,1,2,0:T(8,128)S(1)}, f32[5,32,4,128]{3,1,2,0:T(8,128)}, u32[]{:S(2)}, u32[]{:S(2)}) collective-permute-start(f32[5,32,4,128]{3,1,2,0:T(8,128)S(1)} %copy.253), channel_id=1, source_target_pairs={{1,0},{2,1},{3,2},{16,3},{17,16},{18,17},{19,18},{0,19},{5,4},{6,5... | collective-permute-start | bytes 983048 | tf_op jit(solution)/shard_map/ppermute | solution.py:30
  303.7 8.4 collective-permute-start.16
  303.9 8.8 collective-permute-start.17
  344.5 5.3 collective-permute-start.18
  349.8 44.1 %collective-permute-start.19 = (f32[5,32,4,136]{3,1,2,0:T(8,128)}, f32[5,32,4,136]{3,1,2,0:T(8,128)S(1)}, u32[]{:S(2)}, u32[]{:S(2)}) collective-permute-start(f32[5,32,4,136]{3,1,2,0:T(8,128)} %collective-permute-done.18), channel_id=1, source_target_pairs={{0,8},{4,12},{8,0},{12,4},{1,9},{5,13},{9,1},{13,5},{2,10},{6,14},... | collective-permute-start | bytes 1044488 | tf_op jit(solution)/shard_map/ppermute | solution.py:18
  505.1 29.0 %collective-permute-start = (f32[2,32,4,128]{3,2,0,1:T(4,128)S(1)}, f32[2,32,4,128]{3,2,0,1:T(4,128)S(1)}, u32[]{:S(2)}, u32[]{:S(2)}) collective-permute-start(f32[2,32,4,128]{3,2,0,1:T(4,128)S(1)} %get-tuple-element.547), channel_id=1, source_target_pairs={{1,0},{2,1},{3,2},{16,3},{17,16},{18,17},{19,18},{0,19},{5,4},{6,5... | collective-permute-start | bytes 393224 | tf_op jit(solution)/shard_map/while/body/eval_jaxpr/ppermute | solution.py:30
  506.9 27.2 %collective-permute-start.1 = (f32[2,32,4,128]{3,2,0,1:T(4,128)S(1)}, f32[2,32,4,128]{3,2,0,1:T(4,128)S(1)}, u32[]{:S(2)}, u32[]{:S(2)}) collective-permute-start(f32[2,32,4,128]{3,2,0,1:T(4,128)S(1)} %get-tuple-element.548), channel_id=1, source_target_pairs={{0,1},{1,2},{2,3},{3,16},{16,17},{17,18},{18,19},{19,0},{4,5},{5,6... | collective-permute-start | bytes 393224 | tf_op jit(solution)/shard_map/while/body/eval_jaxpr/ppermute | solution.py:27
  537.6 5.2 collective-permute-start.2
  549.9 8.6 collective-permute-start.5
  583.7 29.0 %collective-permute-start = (f32[2,32,4,128]{3,2,0,1:T(4,128)S(1)}, f32[2,32,4,128]{3,2,0,1:T(4,128)S(1)}, u32[]{:S(2)}, u32[]{:S(2)}) collective-permute-start(f32[2,32,4,128]{3,2,0,1:T(4,128)S(1)} %get-tuple-element.547), channel_id=1, source_target_pairs={{1,0},{2,1},{3,2},{16,3},{17,16},{18,17},{19,18},{0,19},{5,4},{6,5... | collective-permute-start | bytes 393224 | tf_op jit(solution)/shard_map/while/body/eval_jaxpr/ppermute | solution.py:30
  583.7 28.9 %collective-permute-start.1 = (f32[2,32,4,128]{3,2,0,1:T(4,128)S(1)}, f32[2,32,4,128]{3,2,0,1:T(4,128)S(1)}, u32[]{:S(2)}, u32[]{:S(2)}) collective-permute-start(f32[2,32,4,128]{3,2,0,1:T(4,128)S(1)} %get-tuple-element.548), channel_id=1, source_target_pairs={{0,1},{1,2},{2,3},{3,16},{16,17},{17,18},{18,19},{19,0},{4,5},{5,6... | collective-permute-start | bytes 393224 | tf_op jit(solution)/shard_map/while/body/eval_jaxpr/ppermute | solution.py:27
  616.2 5.2 collective-permute-start.2
  628.8 8.5 collective-permute-start.5
  662.5 29.0 %collective-permute-start = (f32[2,32,4,128]{3,2,0,1:T(4,128)S(1)}, f32[2,32,4,128]{3,2,0,1:T(4,128)S(1)}, u32[]{:S(2)}, u32[]{:S(2)}) collective-permute-start(f32[2,32,4,128]{3,2,0,1:T(4,128)S(1)} %get-tuple-element.547), channel_id=1, source_target_pairs={{1,0},{2,1},{3,2},{16,3},{17,16},{18,17},{19,18},{0,19},{5,4},{6,5... | collective-permute-start | bytes 393224 | tf_op jit(solution)/shard_map/while/body/eval_jaxpr/ppermute | solution.py:30
  662.6 28.9 %collective-permute-start.1 = (f32[2,32,4,128]{3,2,0,1:T(4,128)S(1)}, f32[2,32,4,128]{3,2,0,1:T(4,128)S(1)}, u32[]{:S(2)}, u32[]{:S(2)}) collective-permute-start(f32[2,32,4,128]{3,2,0,1:T(4,128)S(1)} %get-tuple-element.548), channel_id=1, source_target_pairs={{0,1},{1,2},{2,3},{3,16},{16,17},{17,18},{18,19},{19,0},{4,5},{5,6... | collective-permute-start | bytes 393224 | tf_op jit(solution)/shard_map/while/body/eval_jaxpr/ppermute | solution.py:27
  707.4 8.5 collective-permute-start.5
  741.1 29.0 %collective-permute-start = (f32[2,32,4,128]{3,2,0,1:T(4,128)S(1)}, f32[2,32,4,128]{3,2,0,1:T(4,128)S(1)}, u32[]{:S(2)}, u32[]{:S(2)}) collective-permute-start(f32[2,32,4,128]{3,2,0,1:T(4,128)S(1)} %get-tuple-element.547), channel_id=1, source_target_pairs={{1,0},{2,1},{3,2},{16,3},{17,16},{18,17},{19,18},{0,19},{5,4},{6,5... | collective-permute-start | bytes 393224 | tf_op jit(solution)/shard_map/while/body/eval_jaxpr/ppermute | solution.py:30
  741.2 28.9 %collective-permute-start.1 = (f32[2,32,4,128]{3,2,0,1:T(4,128)S(1)}, f32[2,32,4,128]{3,2,0,1:T(4,128)S(1)}, u32[]{:S(2)}, u32[]{:S(2)}) collective-permute-start(f32[2,32,4,128]{3,2,0,1:T(4,128)S(1)} %get-tuple-element.548), channel_id=1, source_target_pairs={{0,1},{1,2},{2,3},{3,16},{16,17},{17,18},{18,19},{19,0},{4,5},{5,6... | collective-permute-start | bytes 393224 | tf_op jit(solution)/shard_map/while/body/eval_jaxpr/ppermute | solution.py:27
  786.2 8.5 collective-permute-start.5
  819.9 29.0 %collective-permute-start = (f32[2,32,4,128]{3,2,0,1:T(4,128)S(1)}, f32[2,32,4,128]{3,2,0,1:T(4,128)S(1)}, u32[]{:S(2)}, u32[]{:S(2)}) collective-permute-start(f32[2,32,4,128]{3,2,0,1:T(4,128)S(1)} %get-tuple-element.547), channel_id=1, source_target_pairs={{1,0},{2,1},{3,2},{16,3},{17,16},{18,17},{19,18},{0,19},{5,4},{6,5... | collective-permute-start | bytes 393224 | tf_op jit(solution)/shard_map/while/body/eval_jaxpr/ppermute | solution.py:30
  820.0 28.9 %collective-permute-start.1 = (f32[2,32,4,128]{3,2,0,1:T(4,128)S(1)}, f32[2,32,4,128]{3,2,0,1:T(4,128)S(1)}, u32[]{:S(2)}, u32[]{:S(2)}) collective-permute-start(f32[2,32,4,128]{3,2,0,1:T(4,128)S(1)} %get-tuple-element.548), channel_id=1, source_target_pairs={{0,1},{1,2},{2,3},{3,16},{16,17},{17,18},{18,19},{19,0},{4,5},{5,6... | collective-permute-start | bytes 393224 | tf_op jit(solution)/shard_map/while/body/eval_jaxpr/ppermute | solution.py:27
  864.8 8.5 collective-permute-start.5
  898.5 29.0 %collective-permute-start = (f32[2,32,4,128]{3,2,0,1:T(4,128)S(1)}, f32[2,32,4,128]{3,2,0,1:T(4,128)S(1)}, u32[]{:S(2)}, u32[]{:S(2)}) collective-permute-start(f32[2,32,4,128]{3,2,0,1:T(4,128)S(1)} %get-tuple-element.547), channel_id=1, source_target_pairs={{1,0},{2,1},{3,2},{16,3},{17,16},{18,17},{19,18},{0,19},{5,4},{6,5... | collective-permute-start | bytes 393224 | tf_op jit(solution)/shard_map/while/body/eval_jaxpr/ppermute | solution.py:30
  898.6 28.9 %collective-permute-start.1 = (f32[2,32,4,128]{3,2,0,1:T(4,128)S(1)}, f32[2,32,4,128]{3,2,0,1:T(4,128)S(1)}, u32[]{:S(2)}, u32[]{:S(2)}) collective-permute-start(f32[2,32,4,128]{3,2,0,1:T(4,128)S(1)} %get-tuple-element.548), channel_id=1, source_target_pairs={{0,1},{1,2},{2,3},{3,16},{16,17},{17,18},{18,19},{19,0},{4,5},{5,6... | collective-permute-start | bytes 393224 | tf_op jit(solution)/shard_map/while/body/eval_jaxpr/ppermute | solution.py:27
  943.7 8.5 collective-permute-start.5
  (227 other events, 825.1 us)
where the time goes:
time: 988 us; the launch traced here: 979 us
  other arithmetic  504 us (51%)
  local copies, waits for them, and re-layouts  371 us (38%)
  starting transfers between devices  57.9 us (6%)
  waiting for transfers between devices  41.9 us (4%)
    mul x24, other arithmetic, advance(): grown = center + near[3] * change  109 us
    max x24, other arithmetic, tendency(): jnp.maximum(-north_flow, 0.0) * (north_cells - tracers)  66.4 us
    add x24, other arithmetic, tendency(): change + diffusion * (west_cells + east_cells + south_cells + north_cells...  63.2 us
    scatter-add x1, other arithmetic, local(): blocks = jnp.zeros((4, 9 * ocean_cells), jnp.float32).at[:, places].add(x...  57.2 us
    scatter-add x1, other arithmetic, local(): atmos_flux = jnp.zeros((4, atmos_cells), jnp.float32).at[:, atmos_slots]....  51.3 us
    while x366, local copies, waits for them, and re-layouts  49.6 us
    while x12, local copies, waits for them, and re-layouts, local(): ocean_now = lax.fori_loop(0, ITERS // depth, advance, ocean_tracers)  43.6 us
    gather x2, local copies, waits for them, and re-layouts, local(): sea_vals = jnp.take(nearby, places, axis=1)  40.4 us
  transfers between devices with their start and end apart: 50, of which 15 were waited for; matrix products, arithmetic and copies ran while one was open for 34% of the time, Pallas kernels for 0%

commit v1 on v0

v1 whole, which is shorter than its diff:
```python
import functools

import jax
import jax.numpy as jnp
from jax import lax
from jax.experimental import pallas as pl
from jax.experimental.pallas import tpu as pltpu
from jax.sharding import PartitionSpec as P

ITERS = 24
ATM_SUB = 4
DEPTH = 8

current_scale = 2.0
atmos_gain = 0.5
ocean_gain = 0.02
MESH = pl.DeviceIdType.MESH
F32 = jnp.float32
BF16 = jnp.bfloat16


def bulk_fluxes(air_vals, sea_vals):
    temp_air, humid_air, wind_east, wind_north = air_vals
    sea_temp, current_east, current_north = sea_vals
    shear_east = wind_east - current_east
    shear_north = wind_north - current_north
    wind_speed = jnp.sqrt(shear_east * shear_east + shear_north * shear_north + 0.25)
    richardson = (temp_air - sea_temp) / (wind_speed * wind_speed)
    heat_coeff = 0.1 + 0.4 * jax.nn.sigmoid(-2.0 * richardson)
    drag_coeff = 0.2 + 0.1 * jnp.tanh(wind_speed)
    sensible = heat_coeff * wind_speed * (sea_temp - temp_air)
    latent = heat_coeff * wind_speed * (0.5 * jnp.exp(0.3 * sea_temp) - humid_air)
    return [
        sensible,
        latent,
        drag_coeff * wind_speed * shear_east,
        drag_coeff * wind_speed * shear_north,
    ]


def pieces(value):
    parts = []
    for _ in range(3):
        part = value.astype(BF16)
        parts.append(part)
        value = value - part.astype(F32)
    return parts


def pick(table, onehot_col, onehot_row, rows, fields):
    total = None
    for part in pieces(table):
        term = lax.dot_general(part, onehot_col, (((1,), (0,)), ((), ())), preferred_element_type=F32)
        total = term if total is None else total + term
    return [
        jnp.sum(jnp.where(onehot_row, total[f * rows : (f + 1) * rows], 0.0), axis=0, keepdims=True)
        for f in range(fields)
    ]


def place(values, onehot_col, onehot_row):
    split = [pieces(value) for value in values]
    total = None
    for k in range(3):
        spread = jnp.concatenate(
            [jnp.where(onehot_row, part[k].astype(F32), 0.0) for part in split], axis=0
        ).astype(BF16)
        term = lax.dot_general(spread, onehot_col, (((1,), (1,)), ((), ())), preferred_element_type=F32)
        total = term if total is None else total + term
    return total


def xgrid_kernel(low_ref, near_ref, acell_ref, ocell_ref, w_ref, aflux_ref, oflux_ref, *, rows, cols):
    slots = acell_ref.shape[2]
    bits = cols.bit_length() - 1
    col_iota = lax.broadcasted_iota(jnp.int32, (cols, slots), 0)
    row_iota = lax.broadcasted_iota(jnp.int32, (rows, slots), 0)

    def hots(cell):
        col = jnp.where(col_iota == (cell & (cols - 1)), 1.0, 0.0).astype(BF16)
        return col, row_iota == (cell >> bits)

    acol, arow = hots(acell_ref[0])
    ocol, orow = hots(ocell_ref[0])
    air = pick(low_ref[...], acol, arow, rows, 4)
    sea = pick(near_ref[0], ocol, orow, rows, 3)
    fluxes = bulk_fluxes(air, sea)
    weight_air = w_ref[0, 0]
    weight_sea = w_ref[1, 0]
    mine = place([weight_air * flux for flux in fluxes], acol, arow)

    @pl.when(pl.program_id(0) == 0)
    def _():
        aflux_ref[...] = mine

    @pl.when(pl.program_id(0) > 0)
    def _():
        aflux_ref[...] += mine

    oflux_ref[0] = place([weight_sea * flux for flux in fluxes], ocol, orow)


def xgrid(lowest, nearby, acell, ocell, weights, rows, cols):
    count, _, slots = acell.shape
    return pl.pallas_call(
        functools.partial(xgrid_kernel, rows=rows, cols=cols),
        grid=(count,),
        in_specs=[
            pl.BlockSpec((4 * rows, cols), lambda j: (0, 0)),
            pl.BlockSpec((1, 3 * rows, cols), lambda j: (j, 0, 0)),
            pl.BlockSpec((1, 1, slots), lambda j: (j, 0, 0)),
            pl.BlockSpec((1, 1, slots), lambda j: (j, 0, 0)),
            pl.BlockSpec((2, 1, 1, slots), lambda j: (0, j, 0, 0)),
        ],
        out_specs=[
            pl.BlockSpec((4 * rows, cols), lambda j: (0, 0)),
            pl.BlockSpec((1, 4 * rows, cols), lambda j: (j, 0, 0)),
        ],
        out_shape=[
            jax.ShapeDtypeStruct((4 * rows, cols), F32),
            jax.ShapeDtypeStruct((count, 4 * rows, cols), F32),
        ],
        name="xgrid",
    )(lowest, nearby, acell, ocell, weights)


def atmos_kernel(state_ref, kappa_ref, flux_ref, out_ref):
    levels, rows = state_ref.shape[1], state_ref.shape[2]
    gain = jnp.where(pl.program_id(0) < 2, atmos_gain, -atmos_gain)
    for tile in range(rows // 8):
        at = slice(tile * 8, tile * 8 + 8)
        kappa = kappa_ref[at, :]
        now = [state_ref[0, level, at, :] for level in range(levels)]
        now[0] = now[0] + gain * flux_ref[0, at, :]
        for _ in range(ATM_SUB):
            now = [
                now[l] + kappa * (now[min(l + 1, levels - 1)] + now[max(l - 1, 0)] - 2.0 * now[l])
                for l in range(levels)
            ]
        for level in range(levels):
            out_ref[0, level, at, :] = now[level]


def atmosphere(state, kappa, flux):
    fields, levels, rows, cols = state.shape
    return pl.pallas_call(
        atmos_kernel,
        grid=(fields,),
        in_specs=[
            pl.BlockSpec((1, levels, rows, cols), lambda f: (f, 0, 0, 0)),
            pl.BlockSpec((rows, cols), lambda f: (0, 0)),
            pl.BlockSpec((1, rows, cols), lambda f: (f, 0, 0)),
        ],
        out_specs=pl.BlockSpec((1, levels, rows, cols), lambda f: (f, 0, 0, 0)),
        out_shape=jax.ShapeDtypeStruct(state.shape, F32),
        name="atmosphere",
    )(state, kappa, flux)


def flipped(value, sign):
    rows, cols = value.shape
    for axis, size in ((1, cols), (0, rows)):
        index = lax.broadcasted_iota(jnp.int32, value.shape, axis)
        bit = 1
        while bit < size:
            up = pltpu.roll(value, bit, axis)
            down = pltpu.roll(value, size - bit, axis)
            value = jnp.where((index & bit) == 0, down, up)
            bit *= 2
    return value * sign


def ocean_kernel(
    tr_ref, fl_ref, ka_ref, mask_ref, flux_ref, out_ref,
    st, halo, xt, send_e, send_w, recv_w, recv_e, coef_c, coef_x, force_c, force_x,
    row_send, row_recv, col_send, col_recv,
    *, lat_axes, face_count, gy_count, gx_count,
):
    levels, rows, cols = tr_ref.shape[1], tr_ref.shape[2], tr_ref.shape[3]
    depth = DEPTH
    tall = rows + 2 * depth
    per = cols // depth
    rounds = ITERS // depth
    dyn = 2 * levels
    mask_at = dyn + 3 * levels
    used = mask_at + 3
    groups_all = st.shape[0] // per
    groups_dyn = dyn // per

    face, gy, gx = lax.axis_index("face"), lax.axis_index("gy"), lax.axis_index("gx")
    pos = face * gy_count + gy
    last = face_count * gy_count - 1
    top = pos == last
    n_pos = jnp.where(top, pos, pos + 1)
    n_gx = jnp.where(top, gx_count - 1 - gx, gx)
    s_pos = jnp.where(pos > 0, pos - 1, 0)
    north = {"face": n_pos // gy_count, "gx": n_gx, "gy": n_pos % gy_count}
    south = {"face": s_pos // gy_count, "gx": gx, "gy": s_pos % gy_count}
    east = {"face": face, "gx": (gx + 1) % gx_count, "gy": gy}
    west = {"face": face, "gx": (gx + gx_count - 1) % gx_count, "gy": gy}
    n_slot = jnp.where(top, 1, 0)

    barrier = pltpu.get_barrier_semaphore()
    for where in (north, east, west):
        pl.semaphore_signal(barrier, inc=1, device_id=where, device_id_type=MESH)

    @pl.when(pos > 0)
    def _():
        pl.semaphore_signal(barrier, inc=1, device_id=south, device_id_type=MESH)

    def fill(l, _):
        for t in range(2):
            st[t * levels + l] = tr_ref[t, l]
            st[dyn + t * levels + l] = fl_ref[t, l]
        st[dyn + 2 * levels + l] = ka_ref[l]
        return 0

    lax.fori_loop(0, levels, fill, 0)
    st[mask_at] = mask_ref[...]
    st[mask_at + 1] = -ocean_gain * (flux_ref[0] + flux_ref[1])
    st[mask_at + 2] = ocean_gain * flux_ref[1]
    for plane in range(used, st.shape[0]):
        st[plane] = jnp.zeros((rows, cols), F32)
        for e in range(rounds):
            for s in range(2):
                halo[e, s, plane] = jnp.zeros((depth, cols), F32)

    @pl.when(pos == 0)
    def _():
        def clear(plane, _):
            for e in range(rounds):
                halo[e, 0, plane] = jnp.zeros((depth, cols), F32)
            return 0

        lax.fori_loop(0, used, clear, 0)

    pl.semaphore_wait(barrier, jnp.where(pos > 0, 4, 3))

    lane = lax.broadcasted_iota(jnp.int32, (tall, cols), 1)
    slot = lane // depth

    def column(e, plane):
        return jnp.concatenate([halo[e, 0, plane], st[plane], halo[e, 1, plane]], axis=0)

    def exchange(e, planes, groups):
        up = pltpu.make_async_remote_copy(
            src_ref=st.at[pl.ds(0, planes), pl.ds(rows - depth, depth), :],
            dst_ref=halo.at[e, n_slot, pl.ds(0, planes)],
            send_sem=row_send.at[e, 0], recv_sem=row_recv.at[e, n_slot],
            device_id=north, device_id_type=MESH,
        )
        down = pltpu.make_async_remote_copy(
            src_ref=st.at[pl.ds(0, planes), pl.ds(0, depth), :],
            dst_ref=halo.at[e, 1, pl.ds(0, planes)],
            send_sem=row_send.at[e, 1], recv_sem=row_recv.at[e, 1],
            device_id=south, device_id_type=MESH,
        )
        from_south = pltpu.make_async_remote_copy(
            src_ref=st.at[pl.ds(0, planes), pl.ds(0, depth), :],
            dst_ref=halo.at[e, 0, pl.ds(0, planes)],
            send_sem=row_send.at[e, 1], recv_sem=row_recv.at[e, 0],
            device_id=south, device_id_type=MESH,
        )
        up.start()

        @pl.when(pos > 0)
        def _():
            down.start()
            from_south.wait_recv()
            down.wait_send()

        down.wait_recv()
        up.wait_send()

        @pl.when(top)
        def _():
            def turn(plane, _):
                backward = jnp.logical_and(plane >= dyn, plane < dyn + 2 * levels)
                halo[e, 1, plane] = flipped(halo[e, 1, plane], jnp.where(backward, -1.0, 1.0))
                return 0

            lax.fori_loop(0, planes, turn, 0)

        def pack(g, _):
            to_east = jnp.zeros((tall, cols), F32)
            to_west = jnp.zeros((tall, cols), F32)
            for p in range(per):
                value = column(e, g * per + p)
                here = slot == p
                shift_e = (p + 1) * depth % cols
                moved_e = pltpu.roll(value, shift_e, 1) if shift_e else value
                moved_w = pltpu.roll(value, p * depth, 1) if p else value
                to_east = jnp.where(here, moved_e, to_east)
                to_west = jnp.where(here, moved_w, to_west)
            send_e[e, g] = to_east
            send_w[e, g] = to_west
            return 0

        lax.fori_loop(0, groups, pack, 0)
        go_e = pltpu.make_async_remote_copy(
            src_ref=send_e.at[e, pl.ds(0, groups)], dst_ref=recv_w.at[e, pl.ds(0, groups)],
            send_sem=col_send.at[e, 0], recv_sem=col_recv.at[e, 0],
            device_id=east, device_id_type=MESH,
        )
        go_w = pltpu.make_async_remote_copy(
            src_ref=send_w.at[e, pl.ds(0, groups)], dst_ref=recv_e.at[e, pl.ds(0, groups)],
            send_sem=col_send.at[e, 1], recv_sem=col_recv.at[e, 1],
            device_id=west, device_id_type=MESH,
        )
        go_e.start()
        go_w.start()
        go_e.wait()
        go_w.wait()

        def unpack(g, _):
            for p in range(per):
                from_e = recv_e[e, g]
                from_w = recv_w[e, g]
                shift_w = (cols - depth - p * depth) % cols
                low = pltpu.roll(from_e, cols - p * depth, 1) if p else from_e
                high = pltpu.roll(from_w, shift_w, 1) if shift_w else from_w
                xt[g * per + p] = jnp.where(slot == 0, low, jnp.where(slot == per - 1, high, 0.0))
            return 0

        lax.fori_loop(0, groups, unpack, 0)

    exchange(0, used, groups_all)

    row_index = lax.broadcasted_iota(jnp.int32, (tall, cols), 0)
    floor = jnp.logical_and(row_index == depth, pos == 0)

    def weights(get, out):
        mask = get(mask_at)

        def one(l, _):
            u, v, k = get(dyn + l), get(dyn + levels + l), get(dyn + 2 * levels + l)
            w = mask * (jnp.maximum(u, 0.0) + k)
            e = mask * (jnp.maximum(-u, 0.0) + k)
            s = jnp.where(floor, 0.0, mask * (jnp.maximum(v, 0.0) + k))
            n = mask * (jnp.maximum(-v, 0.0) + k)
            out[0, l] = 1.0 - ((w + e) + (s + n))
            out[1, l] = w
            out[2, l] = e
            out[3, l] = s
            out[4, l] = n
            return 0

        lax.fori_loop(0, levels, one, 0)
        return mask

    centre = functools.partial(column, 0)
    mask_c = weights(centre, coef_c)
    mask_x = weights(lambda plane: xt[plane], coef_x)
    for t in range(2):
        force_c[t] = mask_c * centre(mask_at + 1 + t)
        force_x[t] = mask_x * xt[mask_at + 1 + t]

    first = lane == 0
    final = lane == cols - 1

    def advance(e, l, forced):
        now = [(column(e, t * levels + l), xt[t * levels + l]) for t in range(2)]
        for _ in range(depth):
            later = []
            for t in range(2):
                c, x = now[t]
                rc, rx = pltpu.roll(c, 1, 1), pltpu.roll(x, 1, 1)
                lc, lx = pltpu.roll(c, cols - 1, 1), pltpu.roll(x, cols - 1, 1)
                pair = []
                for mine, w, ea, coef, force in (
                    (c, jnp.where(first, rx, rc), jnp.where(final, lx, lc), coef_c, force_c),
                    (x, jnp.where(first, rc, rx), jnp.where(final, lc, lx), coef_x, force_x),
                ):
                    so = pltpu.roll(mine, 1, 0)
                    no = pltpu.roll(mine, tall - 1, 0)
                    new = coef[0, l] * mine + (coef[1, l] * w + coef[2, l] * ea)
                    new = new + (coef[3, l] * so + coef[4, l] * no)
                    pair.append(new + force[t] if forced else new)
                later.append(tuple(pair))
            now = later
        for t in range(2):
            st[t * levels + l] = now[t][0][depth : depth + rows]

    def round_of(e, _):
        advance(e, 0, True)

        def level(l, _):
            advance(e, l, False)
            return 0

        lax.fori_loop(1, levels, level, 0)

        @pl.when(e < rounds - 1)
        def _():
            exchange(e + 1, dyn, groups_dyn)

        return 0

    lax.fori_loop(0, rounds, round_of, 0)

    def empty(l, _):
        for t in range(2):
            out_ref[t, l] = st[t * levels + l]
        return 0

    lax.fori_loop(0, levels, empty, 0)


def ocean(tracers, flow, kappa, mask, flux):
    _, levels, rows, cols = tracers.shape
    depth = DEPTH
    tall = rows + 2 * depth
    per = cols // depth
    rounds = ITERS // depth
    groups = -(-(5 * levels + 3) // per)
    planes = groups * per
    vm = lambda *shape: pltpu.VMEM(shape, F32)
    return pl.pallas_call(
        functools.partial(
            ocean_kernel, lat_axes=("face", "gy"), face_count=lax.axis_size("face"),
            gy_count=lax.axis_size("gy"), gx_count=lax.axis_size("gx"),
        ),
        in_specs=[pl.BlockSpec(memory_space=pltpu.VMEM)] * 5,
        out_specs=pl.BlockSpec(memory_space=pltpu.VMEM),
        out_shape=jax.ShapeDtypeStruct(tracers.shape, F32),
        scratch_shapes=[
            vm(planes, rows, cols),
            vm(rounds, 2, planes, depth, cols),
            vm(planes, tall, cols),
            vm(rounds, groups, tall, cols),
            vm(rounds, groups, tall, cols),
            vm(rounds, groups, tall, cols),
            vm(rounds, groups, tall, cols),
            vm(5, levels, tall, cols),
            vm(5, levels, tall, cols),
            vm(2, tall, cols),
            vm(2, tall, cols),
            pltpu.SemaphoreType.DMA((rounds, 2)),
            pltpu.SemaphoreType.DMA((rounds, 2)),
            pltpu.SemaphoreType.DMA((rounds, 2)),
            pltpu.SemaphoreType.DMA((rounds, 2)),
        ],
        compiler_params=pltpu.CompilerParams(
            collective_id=0, has_side_effects=True, vmem_limit_bytes=56 * 1024 * 1024
        ),
        name="ocean",
    )(tracers, flow, kappa, mask, flux)


def shifted(value, axis, step, wrap):
    count = lax.axis_size(axis)
    pairs = [(i, (i + step) % count) for i in range(count) if wrap or 0 <= i + step < count]
    return lax.ppermute(value, axis, pairs)


def local(
    atmos_state, atmos_kappa, ocean_tracers, ocean_flow, ocean_kappa, sea_mask,
    xgrid_atmos_cell, xgrid_ocean_cell, xgrid_weights,
):
    rows, cols = ocean_tracers.shape[2], ocean_tracers.shape[3]
    slots = xgrid_atmos_cell.shape[2]
    lat = ("face", "gy")
    lowest = atmos_state[:, 0].reshape(-1, cols)
    surface = jnp.concatenate(
        [ocean_tracers[0, 0], current_scale * ocean_flow[0, 0], current_scale * ocean_flow[1, 0]]
    )[None]
    tall = jnp.concatenate(
        [shifted(surface, lat, 1, False), surface, shifted(surface, lat, -1, False)]
    )
    nearby = jnp.stack([shifted(tall, "gx", 1, True), tall, shifted(tall, "gx", -1, True)], axis=1)
    atmos_flux, blocks = xgrid(
        lowest,
        nearby.reshape(9, 3 * rows, cols),
        xgrid_atmos_cell.reshape(9, 1, slots),
        xgrid_ocean_cell.reshape(9, 1, slots),
        xgrid_weights.reshape(2, 9, 1, slots),
        rows, cols,
    )
    blocks = blocks.reshape(3, 3, 4, rows, cols)
    middle = (
        blocks[1] + shifted(blocks[2], lat, 1, False) + shifted(blocks[0], lat, -1, False)
    )
    ocean_flux = (
        middle[1] + shifted(middle[2], "gx", 1, True) + shifted(middle[0], "gx", -1, True)
    )
    atmos_now = atmosphere(atmos_state, atmos_kappa, atmos_flux.reshape(4, rows, cols))
    sea_weight = sea_mask.astype(F32)
    ocean_now = ocean(ocean_tracers, ocean_flow, ocean_kappa, sea_weight, ocean_flux)
    return (atmos_now, ocean_now, sea_weight * ocean_flux[2:4])


def solution(mesh):
    placed = (
        P(None, None, ("face", "gy"), "gx"),
        P(("face", "gy"), "gx"),
        P(None, None, ("face", "gy"), "gx"),
        P(None, None, ("face", "gy"), "gx"),
        P(None, ("face", "gy"), "gx"),
        P(("face", "gy"), "gx"),
        P(("face", "gy"), "gx", None),
        P(("face", "gy"), "gx", None),
        P(None, ("face", "gy"), "gx", None),
    )
    return jax.shard_map(
        local,
        mesh=mesh,
        in_specs=placed,
        out_specs=(
            P(None, None, ("face", "gy"), "gx"),
            P(None, None, ("face", "gy"), "gx"),
            P(None, ("face", "gy"), "gx"),
        ),
        check_vma=False,
    )
```

time: 988 us -> 341 us (0.35)
  the two profiles are of different devices: /device:TPU:24 before, /device:TPU:27 now
where the time goes in v1:
time: 341 us
  Pallas kernels  302 us (89%)
  waiting for transfers between devices  15.4 us (5%)
  starting transfers between devices  10.8 us (3%)
  local copies, waits for them, and re-layouts  10.2 us (3%)
    pallas_call x1, Pallas kernels, ocean(): pl.pallas_call(functools.partial(ocean_kernel, lat_axes=('face', 'gy'), f...  281 us
    pallas_call x1, Pallas kernels, xgrid(): pl.pallas_call(functools.partial(xgrid_kernel, rows=rows, cols=cols), gri...  17.1 us
    ppermute x8, waiting for transfers between devices, shifted(): return lax.ppermute(value, axis, pairs)  15.4 us
    ppermute x8, starting transfers between devices, shifted(): return lax.ppermute(value, axis, pairs)  10.8 us
  transfers between devices with their start and end apart: 8, of which 3 were waited for; matrix products, arithmetic and copies ran while one was open for 2% of the time, Pallas kernels for 1%

profile of v1, /device:TPU:27, one launch (start us, length us, event | category | flops | bytes accessed | tf_op | source)
XLA Modules:
  0.0 340.8 jit_solution(1995709717529689904)
XLA Ops:
  0.6 0.8 multiply_bitcast_fusion.1
  1.4 2.1 collective-permute-start.1
  3.5 1.3 collective-permute-start
  4.8 0.0 collective-permute-done.1
  4.8 3.7 %collective-permute-done = f32[1,96,128]{2,1,0:T(8,128)S(1)} collective-permute-done((f32[1,96,128]{2,1,0:T(8,128)S(1)}, f32[1,96,128]{2,1,0:T(8,128)S(1)}, u32[]{:S(2)}, u32[]{:S(2)}) %collective-permute-start) | collective-permute-done | bytes 49184 | tf_op jit(solution)/shard_map/ppermute | solution.py:453
  8.6 1.9 collective-permute-start.3
  10.5 1.2 collective-permute-start.2
  11.7 1.5 reshape.34.acell_ref
  13.2 1.5 reshape.35.ocell_ref
  14.6 1.5 slice.36
  16.1 1.6 copy.15.w_ref
  17.7 0.0 collective-permute-done.3
  17.7 0.0 collective-permute-done.2
  17.7 0.0 copy-start.2
  17.7 0.8 copy.14
  18.5 17.1 %xgrid.1 = (f32[128,128]{1,0:T(8,128)}, f32[9,128,128]{2,1,0:T(8,128)}) custom-call(f32[128,128]{1,0:T(8,128)} %bitcast.31, f32[9,96,128]{2,1,0:T(8,128)} %bitcast.29, s32[9,1,1024]{2,1,0:T(1,128)} %reshape.34.acell_ref, s32[9,1,1024]{2,1,0:T(1,128)} %reshape.35.ocell_ref, f32[2,9,1,1024]{3,2,1,0:T(1,128)} %copy.15.w_ref), custom_call_target="tpu_custom_call" | custom-call | tf_op jit(solution)/shard_map/xgrid/pallas_call | solution.py:105
  35.6 1.2 fusion.3
  36.7 2.1 collective-permute-start.5
  38.9 1.3 collective-permute-start.4
  40.2 3.2 collective-permute-done.5
  43.3 8.4 %collective-permute-done.4 = f32[3,4,32,128]{3,2,1,0:T(8,128)S(1)} collective-permute-done((f32[3,4,32,128]{3,2,1,0:T(8,128)S(1)}, f32[3,4,32,128]{3,2,1,0:T(8,128)S(1)}, u32[]{:S(2)}, u32[]{:S(2)}) %collective-permute-start.4) | collective-permute-done | bytes 196640 | tf_op jit(solution)/shard_map/ppermute | solution.py:453
  51.8 0.9 collective-permute-start.6
  52.7 0.0 collective-permute-start.7
  52.7 0.0 copy-done.2
  52.8 0.0 copy-start.1
  52.8 4.4 %atmosphere.1 = f32[4,32,32,128]{3,2,1,0:T(8,128)} custom-call(f32[4,32,32,128]{3,2,1,0:T(8,128)} %state_ref.1, f32[32,128]{1,0:T(8,128)} %kappa_ref.1, f32[4,32,128]{2,1,0:T(8,128)} %bitcast.37), custom_call_target="tpu_custom_call" | custom-call | tf_op jit(solution)/shard_map/atmosphere/pallas_call | solution.py:146
  57.2 0.0 collective-permute-done.6
  57.2 0.0 collective-permute-done.7
  57.2 0.0 copy-start
  57.2 0.6 slice_multiply_fusion
  57.9 280.6 %ocean.1 = f32[2,32,32,128]{3,2,1,0:T(8,128)} custom-call(f32[2,32,32,128]{3,2,1,0:T(8,128)} %tr_ref.1, f32[2,32,32,128]{3,2,1,0:T(8,128)} %fl_ref.1, f32[32,32,128]{2,1,0:T(8,128)} %ka_ref.1, f32[32,128]{1,0:T(8,128)} %copy-done.1, f32[4,32,128]{2,1,0:T(8,128)} %copy-done), custom_call_target="tpu_custom_call" | custom-call | tf_op jit(solution)/shard_map/ocean/pallas_call | solution.py:418
  338.5 2.3 copy.17
  (9 shorter events, 0.1 us)
Async XLA Ops:
  1.4 3.4 collective-permute-start.1
  3.5 5.1 %collective-permute-start = (f32[1,96,128]{2,1,0:T(8,128)S(1)}, f32[1,96,128]{2,1,0:T(8,128)S(1)}, u32[]{:S(2)}, u32[]{:S(2)}) collective-permute-start(f32[1,96,128]{2,1,0:T(8,128)S(1)} %maximum_bitcast_fusion), channel_id=1, source_target_pairs={{0,1},{1,2},{2,3},{3,16},{16,17},{17,18},{18,19},{4,5},{5,6},{6,7}... | collective-permute-start | bytes 147464 | tf_op jit(solution)/shard_map/ppermute | solution.py:453
  8.6 9.1 %collective-permute-start.3 = (f32[3,96,128]{2,1,0:T(8,128)S(1)}, f32[3,96,128]{2,1,0:T(8,128)S(1)}, u32[]{:S(2)}, u32[]{:S(2)}) collective-permute-start(f32[3,96,128]{2,1,0:T(8,128)S(1)} %get-tuple-element.15), channel_id=1, source_target_pairs={{0,12},{4,0},{8,4},{12,8},{1,13},{5,1},{9,5},{13,9},{2,14},{6,2},{... | collective-permute-start | bytes 442376 | tf_op jit(solution)/shard_map/ppermute | solution.py:453
  10.5 7.2 %collective-permute-start.2 = (f32[3,96,128]{2,1,0:T(8,128)S(1)}, f32[3,96,128]{2,1,0:T(8,128)S(1)}, u32[]{:S(2)}, u32[]{:S(2)}) collective-permute-start(f32[3,96,128]{2,1,0:T(8,128)S(1)} %get-tuple-element.15), channel_id=1, source_target_pairs={{0,4},{4,8},{8,12},{12,0},{1,5},{5,9},{9,13},{13,1},{2,6},{6,10},{... | collective-permute-start | bytes 442376 | tf_op jit(solution)/shard_map/ppermute | solution.py:453
  17.7 35.0 %copy-start.2 = (s32[32,128]{1,0:T(8,128)S(1)}, s32[32,128]{1,0:T(8,128)}, u32[]{:S(2)}) copy-start(s32[32,128]{1,0:T(8,128)} %param.14) | copy-start | bytes 49156
  36.7 6.6 %collective-permute-start.5 = (f32[3,4,32,128]{3,2,1,0:T(8,128)S(1)}, f32[3,4,32,128]{3,2,1,0:T(8,128)S(1)}, u32[]{:S(2)}, u32[]{:S(2)}) collective-permute-start(f32[3,4,32,128]{3,2,1,0:T(8,128)S(1)} %bitcast.33), channel_id=1, source_target_pairs={{1,0},{2,1},{3,2},{16,3},{17,16},{18,17},{19,18},{5,4},{6,5},{7,6}... | collective-permute-start | bytes 589832 | tf_op jit(solution)/shard_map/ppermute | solution.py:453
  38.9 12.9 %collective-permute-start.4 = (f32[3,4,32,128]{3,2,1,0:T(8,128)S(1)}, f32[3,4,32,128]{3,2,1,0:T(8,128)S(1)}, u32[]{:S(2)}, u32[]{:S(2)}) collective-permute-start(f32[3,4,32,128]{3,2,1,0:T(8,128)S(1)} %bitcast.32), channel_id=1, source_target_pairs={{0,1},{1,2},{2,3},{3,16},{16,17},{17,18},{18,19},{4,5},{5,6},{6,7}... | collective-permute-start | bytes 589832 | tf_op jit(solution)/shard_map/ppermute | solution.py:453
  51.8 5.3 %collective-permute-start.6 = (f32[4,32,128]{2,1,0:T(8,128)S(1)}, f32[4,32,128]{2,1,0:T(8,128)S(1)}, u32[]{:S(2)}, u32[]{:S(2)}) collective-permute-start(f32[4,32,128]{2,1,0:T(8,128)S(1)} %get-tuple-element.12), channel_id=1, source_target_pairs={{0,4},{4,8},{8,12},{12,0},{1,5},{5,9},{9,13},{13,1},{2,6},{6,10},{... | collective-permute-start | bytes 196616 | tf_op jit(solution)/shard_map/ppermute | solution.py:453
  52.7 4.5 %collective-permute-start.7 = (f32[4,32,128]{2,1,0:T(8,128)S(1)}, f32[4,32,128]{2,1,0:T(8,128)S(1)}, u32[]{:S(2)}, u32[]{:S(2)}) collective-permute-start(f32[4,32,128]{2,1,0:T(8,128)S(1)} %get-tuple-element.13), channel_id=1, source_target_pairs={{0,12},{4,0},{8,4},{12,8},{1,13},{5,1},{9,5},{13,9},{2,14},{6,2},{... | collective-permute-start | bytes 196616 | tf_op jit(solution)/shard_map/ppermute | solution.py:453
  52.8 4.5 %copy-start.1 = (f32[32,128]{1,0:T(8,128)}, f32[32,128]{1,0:T(8,128)S(1)}, u32[]{:S(2)}) copy-start(f32[32,128]{1,0:T(8,128)S(1)} %convert_element_type.3.mask_ref) | copy-start | bytes 49156
  57.2 0.6 copy-start

commit v2 on v1

v2 whole, which is shorter than its diff:
```python
import functools

import jax
import jax.numpy as jnp
from jax import lax
from jax.experimental import pallas as pl
from jax.experimental.pallas import tpu as pltpu
from jax.sharding import PartitionSpec as P

ITERS = 24
ATM_SUB = 4
DEPTH = 8

current_scale = 2.0
atmos_gain = 0.5
ocean_gain = 0.02
MESH = pl.DeviceIdType.MESH
F32 = jnp.float32
BF16 = jnp.bfloat16


def bulk_fluxes(air_vals, sea_vals):
    temp_air, humid_air, wind_east, wind_north = air_vals
    sea_temp, current_east, current_north = sea_vals
    shear_east = wind_east - current_east
    shear_north = wind_north - current_north
    wind_speed = jnp.sqrt(shear_east * shear_east + shear_north * shear_north + 0.25)
    richardson = (temp_air - sea_temp) / (wind_speed * wind_speed)
    heat_coeff = 0.1 + 0.4 * jax.nn.sigmoid(-2.0 * richardson)
    drag_coeff = 0.2 + 0.1 * jnp.tanh(wind_speed)
    sensible = heat_coeff * wind_speed * (sea_temp - temp_air)
    latent = heat_coeff * wind_speed * (0.5 * jnp.exp(0.3 * sea_temp) - humid_air)
    return [
        sensible,
        latent,
        drag_coeff * wind_speed * shear_east,
        drag_coeff * wind_speed * shear_north,
    ]


def pieces(value):
    parts = []
    for _ in range(3):
        part = value.astype(BF16)
        parts.append(part)
        value = value - part.astype(F32)
    return parts


def pick(table, onehot_col, onehot_row, rows, fields):
    total = None
    for part in pieces(table):
        term = lax.dot_general(part, onehot_col, (((1,), (0,)), ((), ())), preferred_element_type=F32)
        total = term if total is None else total + term
    return [
        jnp.sum(jnp.where(onehot_row, total[f * rows : (f + 1) * rows], 0.0), axis=0, keepdims=True)
        for f in range(fields)
    ]


def place(values, onehot_col, onehot_row):
    split = [pieces(value) for value in values]
    total = None
    for k in range(3):
        spread = jnp.concatenate(
            [jnp.where(onehot_row, part[k].astype(F32), 0.0) for part in split], axis=0
        ).astype(BF16)
        term = lax.dot_general(spread, onehot_col, (((1,), (1,)), ((), ())), preferred_element_type=F32)
        total = term if total is None else total + term
    return total


def xgrid_kernel(low_ref, near_ref, acell_ref, ocell_ref, w_ref, aflux_ref, oflux_ref, *, rows, cols):
    slots = acell_ref.shape[2]
    bits = cols.bit_length() - 1
    col_iota = lax.broadcasted_iota(jnp.int32, (cols, slots), 0)
    row_iota = lax.broadcasted_iota(jnp.int32, (rows, slots), 0)

    def hots(cell):
        col = jnp.where(col_iota == (cell & (cols - 1)), 1.0, 0.0).astype(BF16)
        return col, row_iota == (cell >> bits)

    acol, arow = hots(acell_ref[0])
    ocol, orow = hots(ocell_ref[0])
    air = pick(low_ref[...], acol, arow, rows, 4)
    sea = pick(near_ref[0], ocol, orow, rows, 3)
    fluxes = bulk_fluxes(air, sea)
    weight_air = w_ref[0, 0]
    weight_sea = w_ref[1, 0]
    mine = place([weight_air * flux for flux in fluxes], acol, arow)

    @pl.when(pl.program_id(0) == 0)
    def _():
        aflux_ref[...] = mine

    @pl.when(pl.program_id(0) > 0)
    def _():
        aflux_ref[...] += mine

    oflux_ref[0] = place([weight_sea * flux for flux in fluxes], ocol, orow)


def xgrid(lowest, nearby, acell, ocell, weights, rows, cols):
    count, _, slots = acell.shape
    return pl.pallas_call(
        functools.partial(xgrid_kernel, rows=rows, cols=cols),
        grid=(count,),
        in_specs=[
            pl.BlockSpec((4 * rows, cols), lambda j: (0, 0)),
            pl.BlockSpec((1, 3 * rows, cols), lambda j: (j, 0, 0)),
            pl.BlockSpec((1, 1, slots), lambda j: (j, 0, 0)),
            pl.BlockSpec((1, 1, slots), lambda j: (j, 0, 0)),
            pl.BlockSpec((2, 1, 1, slots), lambda j: (0, j, 0, 0)),
        ],
        out_specs=[
            pl.BlockSpec((4 * rows, cols), lambda j: (0, 0)),
            pl.BlockSpec((1, 4 * rows, cols), lambda j: (j, 0, 0)),
        ],
        out_shape=[
            jax.ShapeDtypeStruct((4 * rows, cols), F32),
            jax.ShapeDtypeStruct((count, 4 * rows, cols), F32),
        ],
        name="xgrid",
    )(lowest, nearby, acell, ocell, weights)


def atmos_kernel(state_ref, kappa_ref, flux_ref, out_ref):
    levels, rows = state_ref.shape[1], state_ref.shape[2]
    gain = jnp.where(pl.program_id(0) < 2, atmos_gain, -atmos_gain)
    for tile in range(rows // 8):
        at = slice(tile * 8, tile * 8 + 8)
        kappa = kappa_ref[at, :]
        now = [state_ref[0, level, at, :] for level in range(levels)]
        now[0] = now[0] + gain * flux_ref[0, at, :]
        for _ in range(ATM_SUB):
            now = [
                now[l] + kappa * (now[min(l + 1, levels - 1)] + now[max(l - 1, 0)] - 2.0 * now[l])
                for l in range(levels)
            ]
        for level in range(levels):
            out_ref[0, level, at, :] = now[level]


def atmosphere(state, kappa, flux):
    fields, levels, rows, cols = state.shape
    return pl.pallas_call(
        atmos_kernel,
        grid=(fields,),
        in_specs=[
            pl.BlockSpec((1, levels, rows, cols), lambda f: (f, 0, 0, 0)),
            pl.BlockSpec((rows, cols), lambda f: (0, 0)),
            pl.BlockSpec((1, rows, cols), lambda f: (f, 0, 0)),
        ],
        out_specs=pl.BlockSpec((1, levels, rows, cols), lambda f: (f, 0, 0, 0)),
        out_shape=jax.ShapeDtypeStruct(state.shape, F32),
        name="atmosphere",
    )(state, kappa, flux)


def mirror(value):
    cols = value.shape[1]
    row = lax.broadcasted_iota(jnp.int32, (cols, cols), 0)
    col = lax.broadcasted_iota(jnp.int32, (cols, cols), 1)
    swap = jnp.where(row + col == cols - 1, 1.0, 0.0).astype(BF16)
    total = None
    for part in pieces(value):
        term = jnp.dot(part, swap, preferred_element_type=F32)
        total = term if total is None else total + term
    return total


def ocean_kernel(
    all_ref, misc_ref, st,
    halo0, halo_m, halo1, send0, recv0, send1, recv1, xt0, ping, pong, coef, force,
    row0_send, row0_recv, misc_send, misc_recv, col0_send, col0_recv,
    row_send, row_recv, col_send, col_recv,
    *, face_count, gy_count, gx_count,
):
    rows, groups, sub, cols = all_ref.shape
    chunks = groups // 5
    depth = DEPTH
    tall = rows + 2 * depth
    per = cols // depth
    packs = tall // per
    rounds = ITERS // depth
    end = depth + rows

    face, gy, gx = lax.axis_index("face"), lax.axis_index("gy"), lax.axis_index("gx")
    pos = face * gy_count + gy
    last = face_count * gy_count - 1
    top = pos == last
    n_pos = jnp.where(top, pos, pos + 1)
    n_gx = jnp.where(top, gx_count - 1 - gx, gx)
    s_pos = jnp.where(pos > 0, pos - 1, 0)
    north = {"face": n_pos // gy_count, "gx": n_gx, "gy": n_pos % gy_count}
    south = {"face": s_pos // gy_count, "gx": gx, "gy": s_pos % gy_count}
    east = {"face": face, "gx": (gx + 1) % gx_count, "gy": gy}
    west = {"face": face, "gx": (gx + gx_count - 1) % gx_count, "gy": gy}
    n_slot = jnp.where(top, 1, 0)

    barrier = pltpu.get_barrier_semaphore()
    for where in (north, east, west):
        pl.semaphore_signal(barrier, inc=1, device_id=where, device_id_type=MESH)

    @pl.when(pos > 0)
    def _():
        pl.semaphore_signal(barrier, inc=1, device_id=south, device_id_type=MESH)

    @pl.when(pos == 0)
    def _():
        def clear(r, _):
            halo0[0, r] = jnp.zeros((groups, sub, cols), F32)
            halo_m[0, r] = jnp.zeros((sub, cols), F32)
            for e in range(rounds - 1):
                for c in range(chunks):
                    halo1[e, c, 0, r] = jnp.zeros((2, sub, cols), F32)
            return 0

        lax.fori_loop(0, depth, clear, 0)

    pl.semaphore_wait(barrier, jnp.where(pos > 0, 4, 3))

    def remote(src, dst, send, recv, device):
        return pltpu.make_async_remote_copy(
            src_ref=src, dst_ref=dst, send_sem=send, recv_sem=recv,
            device_id=device, device_id_type=MESH,
        )

    def row_copies(high, low, halo_of, send, recv):
        up = remote(high, halo_of(n_slot), send(0), recv(n_slot), north)
        down = remote(low, halo_of(1), send(1), recv(1), south)
        below = remote(low, halo_of(0), send(1), recv(0), south)
        return up, down, below

    def begin(copies):
        copies[0].start()

        @pl.when(pos > 0)
        def _():
            copies[1].start()

    def finish(copies):
        up, down, below = copies

        @pl.when(pos > 0)
        def _():
            below.wait_recv()
            down.wait_send()

        down.wait_recv()
        up.wait_send()

    lane = lax.broadcasted_iota(jnp.int32, (sub, cols), 1)
    slot = lane // depth
    first = lane == 0
    final = lane == cols - 1

    def packed(value_of):
        to_east, to_west = None, None
        for p in range(per):
            value = value_of(p)
            shift_e = (p + 1) * depth % cols
            moved_e = pltpu.roll(value, shift_e, 1) if shift_e else value
            moved_w = pltpu.roll(value, p * depth, 1) if p else value
            to_east = moved_e if p == 0 else jnp.where(slot == p, moved_e, to_east)
            to_west = moved_w if p == 0 else jnp.where(slot == p, moved_w, to_west)
        return to_east, to_west

    def unpacked(from_w, from_e, p):
        shift_w = (cols - depth - p * depth) % cols
        low = pltpu.roll(from_e, cols - p * depth, 1) if p else from_e
        high = pltpu.roll(from_w, shift_w, 1) if shift_w else from_w
        return jnp.where(slot == 0, low, jnp.where(slot == per - 1, high, 0.0))

    rows0 = row_copies(
        all_ref.at[pl.ds(rows - depth, depth)], all_ref.at[pl.ds(0, depth)],
        lambda s: halo0.at[s], lambda s: row0_send.at[s], lambda s: row0_recv.at[s],
    )
    rows_m = row_copies(
        misc_ref.at[pl.ds(rows - depth, depth)], misc_ref.at[pl.ds(0, depth)],
        lambda s: halo_m.at[s], lambda s: misc_send.at[s], lambda s: misc_recv.at[s],
    )
    begin(rows0)
    begin(rows_m)
    finish(rows0)
    finish(rows_m)

    @pl.when(top)
    def _():
        kind = (lax.broadcasted_iota(jnp.int32, (groups * sub, cols), 0) // sub) % 5
        sign = jnp.where(jnp.logical_or(kind == 2, kind == 3), -1.0, 1.0)

        def turn(i, _):
            j = depth - 1 - i
            a = mirror(halo0[1, i].reshape(groups * sub, cols)) * sign
            b = mirror(halo0[1, j].reshape(groups * sub, cols)) * sign
            halo0[1, i] = b.reshape(groups, sub, cols)
            halo0[1, j] = a.reshape(groups, sub, cols)
            return 0

        lax.fori_loop(0, depth // 2, turn, 0)
        turned = mirror(halo_m[1].reshape(depth * sub, cols)).reshape(depth, sub, cols)
        for i in range(depth):
            halo_m[1, i] = turned[depth - 1 - i]

    def row0(r, g):
        if r < depth:
            return halo0[0, r, g]
        if r < end:
            return all_ref[r - depth, g]
        return halo0[1, r - end, g]

    def row_m(r):
        if r < depth:
            return halo_m[0, r]
        if r < end:
            return misc_ref[r - depth]
        return halo_m[1, r - end]

    def pack0(g, _):
        for k in range(packs):
            send0[0, g, k], send0[1, g, k] = packed(lambda p: row0(k * per + p, g))
        return 0

    lax.fori_loop(0, groups, pack0, 0)
    for k in range(packs):
        send0[0, groups, k], send0[1, groups, k] = packed(lambda p: row_m(k * per + p))
    go_e = remote(send0.at[0], recv0.at[0], col0_send.at[0], col0_recv.at[0], east)
    go_w = remote(send0.at[1], recv0.at[1], col0_send.at[1], col0_recv.at[1], west)
    go_e.start()
    go_w.start()

    def weights(tile, get, get_m):
        def fields(c, _):
            for r in range(tall):
                mask = jnp.broadcast_to(get_m(r)[2:3], (sub, cols))
                u, v, k = get(r, c * 5 + 2), get(r, c * 5 + 3), get(r, c * 5 + 4)
                w = mask * (jnp.maximum(u, 0.0) + k)
                e = mask * (jnp.maximum(-u, 0.0) + k)
                s = mask * (jnp.maximum(v, 0.0) + k)
                if r == depth:
                    s = jnp.where(pos == 0, 0.0, 1.0) * s
                n = mask * (jnp.maximum(-v, 0.0) + k)
                coef[c, tile, r, 0] = 1.0 - ((w + e) + (s + n))
                coef[c, tile, r, 1] = w
                coef[c, tile, r, 2] = e
                coef[c, tile, r, 3] = s
                coef[c, tile, r, 4] = n
            return 0

        lax.fori_loop(0, chunks, fields, 0)
        level = lax.broadcasted_iota(jnp.int32, (sub, cols), 0)
        for r in range(tall):
            misc = get_m(r)
            for t in range(2):
                force[t, tile, r] = jnp.where(level == 0, misc[2:3] * misc[t : t + 1], 0.0)

    weights(0, row0, row_m)
    go_e.wait()
    go_w.wait()

    def unpack0(g, _):
        for k in range(packs):
            from_w, from_e = recv0[0, g, k], recv0[1, g, k]
            for p in range(per):
                xt0[k * per + p, g] = unpacked(from_w, from_e, p)
        return 0

    lax.fori_loop(0, groups + 1, unpack0, 0)
    weights(1, lambda r, g: xt0[r, g], lambda r: xt0[r, groups])

    def chunk_rows(e, c):
        return row_copies(
            st.at[pl.ds(rows - depth, depth), pl.ds(2 * c, 2)],
            st.at[pl.ds(0, depth), pl.ds(2 * c, 2)],
            lambda s: halo1.at[e, c, s], lambda s: row_send.at[e, c, s], lambda s: row_recv.at[e, c, s],
        )

    def chunk_cols(e, c):
        return (
            remote(send1.at[e, c, 0], recv1.at[e, c, 0], col_send.at[e, c, 0], col_recv.at[e, c, 0], east),
            remote(send1.at[e, c, 1], recv1.at[e, c, 1], col_send.at[e, c, 1], col_recv.at[e, c, 1], west),
        )

    def row1(e, c, r, t):
        if r < depth:
            return halo1[e, c, 0, r, t]
        if r < end:
            return st[r - depth, 2 * c + t]
        return halo1[e, c, 1, r - end, t]

    def pass_on(e, c):
        finish(chunk_rows(e, c))

        @pl.when(top)
        def _():
            whole = halo1[e, c, 1].reshape(depth * 2 * sub, cols)
            turned = mirror(whole).reshape(depth, 2, sub, cols)
            for i in range(depth):
                halo1[e, c, 1, i] = turned[depth - 1 - i]

        for t in range(2):
            for k in range(packs):
                to_east, to_west = packed(lambda p: row1(e, c, k * per + p, t))
                send1[e, c, 0, t, k] = to_east
                send1[e, c, 1, t, k] = to_west
        for copy in chunk_cols(e, c):
            copy.start()

    def collect(e, c):
        for copy in chunk_cols(e, c):
            copy.wait()
        for t in range(2):
            for k in range(packs):
                from_w, from_e = recv1[e, c, 0, t, k], recv1[e, c, 1, t, k]
                for p in range(per):
                    ping[1, k * per + p, t] = unpacked(from_w, from_e, p)
            for r in range(tall):
                ping[0, r, t] = row1(e, c, r, t)

    def steps(c):
        for s in range(depth):
            src, dst = (ping, pong) if s % 2 == 0 else (pong, ping)
            done = s == depth - 1
            for r in range(s + 1, tall - 1 - s):
                for t in range(2):
                    centre, extra = src[0, r, t], src[1, r, t]
                    rc, rx = pltpu.roll(centre, 1, 1), pltpu.roll(extra, 1, 1)
                    lc, lx = pltpu.roll(centre, cols - 1, 1), pltpu.roll(extra, cols - 1, 1)
                    tiles = (
                        (centre, jnp.where(first, rx, rc), jnp.where(final, lx, lc)),
                        (extra, jnp.where(first, rc, rx), jnp.where(final, lc, lx)),
                    )
                    for i, (mine, w, e) in enumerate(tiles[:1] if done else tiles):
                        new = coef[c, i, r, 0] * mine + (coef[c, i, r, 1] * w + coef[c, i, r, 2] * e)
                        new = new + (
                            coef[c, i, r, 3] * src[i, r - 1, t] + coef[c, i, r, 4] * src[i, r + 1, t]
                        )
                        if done:
                            st[r - depth, 2 * c + t] = new
                        else:
                            dst[i, r, t] = new

            @pl.when(c == 0)
            def _():
                for r in range(s + 1, tall - 1 - s):
                    for t in range(2):
                        if done:
                            st[r - depth, t] += force[t, 0, r]
                        else:
                            dst[0, r, t] += force[t, 0, r]
                            dst[1, r, t] += force[t, 1, r]

    def item(i, _):
        e, c = i // chunks, i % chunks

        @pl.when(e == 0)
        def _():
            for r in range(tall):
                for t in range(2):
                    ping[0, r, t] = row0(r, c * 5 + t)
                    ping[1, r, t] = xt0[r, c * 5 + t]

        @pl.when(e > 0)
        def _():
            collect(e - 1, c)

        steps(c)

        @pl.when(e < rounds - 1)
        def _():
            begin(chunk_rows(e, c))

        j = i - 1

        @pl.when(jnp.logical_and(j >= 0, j < (rounds - 1) * chunks))
        def _():
            pass_on(j // chunks, j % chunks)

        return 0

    lax.fori_loop(0, rounds * chunks, item, 0)


def ocean(fields, misc):
    rows, groups, sub, cols = fields.shape
    chunks = groups // 5
    depth = DEPTH
    tall = rows + 2 * depth
    packs = tall * depth // cols
    later = ITERS // depth - 1
    vm = lambda *shape: pltpu.VMEM((*shape, sub, cols), F32)
    dma = lambda *shape: pltpu.SemaphoreType.DMA(shape)
    return pl.pallas_call(
        functools.partial(
            ocean_kernel, face_count=lax.axis_size("face"),
            gy_count=lax.axis_size("gy"), gx_count=lax.axis_size("gx"),
        ),
        in_specs=[pl.BlockSpec(memory_space=pltpu.VMEM)] * 2,
        out_specs=pl.BlockSpec(memory_space=pltpu.VMEM),
        out_shape=jax.ShapeDtypeStruct((rows, 2 * chunks, sub, cols), F32),
        scratch_shapes=[
            vm(2, depth, groups),
            vm(2, depth),
            vm(later, chunks, 2, depth, 2),
            vm(2, groups + 1, packs),
            vm(2, groups + 1, packs),
            vm(later, chunks, 2, 2, packs),
            vm(later, chunks, 2, 2, packs),
            vm(tall, groups + 1),
            vm(2, tall, 2),
            vm(2, tall, 2),
            vm(chunks, 2, tall, 5),
            vm(2, 2, tall),
            dma(2), dma(2), dma(2), dma(2), dma(2), dma(2),
            dma(later, chunks, 2), dma(later, chunks, 2), dma(later, chunks, 2), dma(later, chunks, 2),
        ],
        compiler_params=pltpu.CompilerParams(
            collective_id=0, has_side_effects=True, vmem_limit_bytes=48 * 1024 * 1024
        ),
        name="ocean",
    )(fields, misc)


def shifted(value, axis, step, wrap):
    count = lax.axis_size(axis)
    pairs = [(i, (i + step) % count) for i in range(count) if wrap or 0 <= i + step < count]
    return lax.ppermute(value, axis, pairs)


def local(
    atmos_state, atmos_kappa, ocean_tracers, ocean_flow, ocean_kappa, sea_mask,
    xgrid_atmos_cell, xgrid_ocean_cell, xgrid_weights,
):
    rows, cols = ocean_tracers.shape[2], ocean_tracers.shape[3]
    slots = xgrid_atmos_cell.shape[2]
    lat = ("face", "gy")
    lowest = atmos_state[:, 0].reshape(-1, cols)
    surface = jnp.concatenate(
        [ocean_tracers[0, 0], current_scale * ocean_flow[0, 0], current_scale * ocean_flow[1, 0]]
    )[None]
    tall = jnp.concatenate(
        [shifted(surface, lat, 1, False), surface, shifted(surface, lat, -1, False)]
    )
    nearby = jnp.stack([shifted(tall, "gx", 1, True), tall, shifted(tall, "gx", -1, True)], axis=1)
    atmos_flux, blocks = xgrid(
        lowest,
        nearby.reshape(9, 3 * rows, cols),
        xgrid_atmos_cell.reshape(9, 1, slots),
        xgrid_ocean_cell.reshape(9, 1, slots),
        xgrid_weights.reshape(2, 9, 1, slots),
        rows, cols,
    )
    blocks = blocks.reshape(3, 3, 4, rows, cols)
    middle = (
        blocks[1] + shifted(blocks[2], lat, 1, False) + shifted(blocks[0], lat, -1, False)
    )
    ocean_flux = (
        middle[1] + shifted(middle[2], "gx", 1, True) + shifted(middle[0], "gx", -1, True)
    )
    atmos_now = atmosphere(atmos_state, atmos_kappa, atmos_flux.reshape(4, rows, cols))
    sea_weight = sea_mask.astype(F32)
    levels = ocean_tracers.shape[1]
    fields = jnp.concatenate([ocean_tracers, ocean_flow, ocean_kappa[None]])
    fields = fields.reshape(5, levels // 8, 8, rows, cols).transpose(3, 1, 0, 2, 4)
    fields = fields.reshape(rows, 5 * levels // 8, 8, cols)
    forcing = jnp.stack(
        [-ocean_gain * (ocean_flux[0] + ocean_flux[1]), ocean_gain * ocean_flux[1], sea_weight], axis=1
    )
    misc = jnp.pad(forcing, ((0, 0), (0, 5), (0, 0)))
    ocean_now = ocean(fields, misc).reshape(rows, levels // 8, 2, 8, cols)
    ocean_now = ocean_now.transpose(2, 1, 3, 0, 4).reshape(ocean_tracers.shape)
    return (atmos_now, ocean_now, sea_weight * ocean_flux[2:4])


def solution(mesh):
    placed = (
        P(None, None, ("face", "gy"), "gx"),
        P(("face", "gy"), "gx"),
        P(None, None, ("face", "gy"), "gx"),
        P(None, None, ("face", "gy"), "gx"),
        P(None, ("face", "gy"), "gx"),
        P(("face", "gy"), "gx"),
        P(("face", "gy"), "gx", None),
        P(("face", "gy"), "gx", None),
        P(None, ("face", "gy"), "gx", None),
    )
    return jax.shard_map(
        local,
        mesh=mesh,
        in_specs=placed,
        out_specs=(
            P(None, None, ("face", "gy"), "gx"),
            P(None, None, ("face", "gy"), "gx"),
            P(None, ("face", "gy"), "gx"),
        ),
        check_vma=False,
    )
```

time: 341 us -> 164 us (0.48)
  the two profiles are of different devices: /device:TPU:27 before, /device:TPU:24 now
where the time goes in v2:
time: 164 us; the launch traced here: 163 us
  Pallas kernels  125 us (76%)
  starting transfers between devices  19.8 us (12%)
  local copies, waits for them, and re-layouts  11.1 us (7%)
  waiting for transfers between devices  5.21 us (3%)
  other arithmetic  1.86 us (1%)
    pallas_call x1, Pallas kernels, ocean(): pl.pallas_call(functools.partial(ocean_kernel, face_count=lax.axis_size('...  103 us
    ppermute x8, starting transfers between devices, shifted(): return lax.ppermute(value, axis, pairs)  19.8 us
    pallas_call x1, Pallas kernels, xgrid(): pl.pallas_call(functools.partial(xgrid_kernel, rows=rows, cols=cols), gri...  17.1 us
    ppermute x8, waiting for transfers between devices, shifted(): return lax.ppermute(value, axis, pairs)  5.21 us
    pallas_call x1, Pallas kernels, atmosphere(): pl.pallas_call(atmos_kernel, grid=(fields,), in_specs=[pl.BlockSpec((1, l...  4.42 us
  transfers between devices with their start and end apart: 8, of which 4 were waited for; matrix products, arithmetic and copies ran while one was open for 5% of the time, Pallas kernels for 3%

profile of v2, /device:TPU:24, one launch (start us, length us, event | category | flops | bytes accessed | tf_op | source)
XLA Modules:
  0.0 163.4 jit_solution(6523191757357794036)
XLA Ops:
  0.6 0.8 multiply_bitcast_fusion.1
  1.5 2.4 %collective-permute-start.1 = (f32[1,96,128]{2,1,0:T(8,128)S(1)}, f32[1,96,128]{2,1,0:T(8,128)S(1)}, u32[]{:S(2)}, u32[]{:S(2)}) collective-permute-start(f32[1,96,128]{2,1,0:T(8,128)S(1)} %maximum_bitcast_fusion), channel_id=1, source_target_pairs={{1,0},{2,1},{3,2},{16,3},{17,16},{18,17},{19,18},{5,4},{6,5},{7,6}... | collective-permute-start | bytes 147464 | tf_op jit(solution)/shard_map/ppermute | solution.py:528
  3.8 6.2 %collective-permute-start = (f32[1,96,128]{2,1,0:T(8,128)S(1)}, f32[1,96,128]{2,1,0:T(8,128)S(1)}, u32[]{:S(2)}, u32[]{:S(2)}) collective-permute-start(f32[1,96,128]{2,1,0:T(8,128)S(1)} %maximum_bitcast_fusion), channel_id=1, source_target_pairs={{0,1},{1,2},{2,3},{3,16},{16,17},{17,18},{18,19},{4,5},{5,6},{6,7}... | collective-permute-start | bytes 147464 | tf_op jit(solution)/shard_map/ppermute | solution.py:528
  10.0 0.1 collective-permute-done.1
  10.1 1.6 collective-permute-done
  11.8 0.0 copy-start
  11.8 0.1 collective-permute-start.3
  11.9 0.5 collective-permute-start.2
  12.3 1.5 reshape.83.acell_ref
  13.8 1.5 reshape.84.ocell_ref
  15.3 1.5 slice.43
  16.8 1.6 copy.20.w_ref
  18.4 0.8 copy.19
  19.2 17.1 %xgrid.1 = (f32[128,128]{1,0:T(8,128)}, f32[9,128,128]{2,1,0:T(8,128)}) custom-call(f32[128,128]{1,0:T(8,128)} %bitcast.52, f32[9,96,128]{2,1,0:T(8,128)} %bitcast.46, s32[9,1,1024]{2,1,0:T(1,128)} %reshape.83.acell_ref, s32[9,1,1024]{2,1,0:T(1,128)} %reshape.84.ocell_ref, f32[2,9,1,1024]{3,2,1,0:T(1,128)} %copy.20.w_ref), custom_call_target="tpu_custom_call" | custom-call | tf_op jit(solution)/shard_map/xgrid/pallas_call | solution.py:105
  36.3 1.2 fusion.4
  37.5 1.9 %collective-permute-start.5 = (f32[3,4,32,128]{3,2,1,0:T(8,128)S(1)}, f32[3,4,32,128]{3,2,1,0:T(8,128)S(1)}, u32[]{:S(2)}, u32[]{:S(2)}) collective-permute-start(f32[3,4,32,128]{3,2,1,0:T(8,128)S(1)} %bitcast.54), channel_id=1, source_target_pairs={{1,0},{2,1},{3,2},{16,3},{17,16},{18,17},{19,18},{5,4},{6,5},{7,6}... | collective-permute-start | bytes 589832 | tf_op jit(solution)/shard_map/ppermute | solution.py:528
  39.4 6.9 %collective-permute-start.4 = (f32[3,4,32,128]{3,2,1,0:T(8,128)S(1)}, f32[3,4,32,128]{3,2,1,0:T(8,128)S(1)}, u32[]{:S(2)}, u32[]{:S(2)}) collective-permute-start(f32[3,4,32,128]{3,2,1,0:T(8,128)S(1)} %bitcast.53), channel_id=1, source_target_pairs={{0,1},{1,2},{2,3},{3,16},{16,17},{17,18},{18,19},{4,5},{5,6},{6,7}... | collective-permute-start | bytes 589832 | tf_op jit(solution)/shard_map/ppermute | solution.py:528
  46.4 0.3 copy.23
  46.7 0.6 copy.22
  47.3 0.6 copy.21
  47.9 1.9 %collective-permute-done.5 = f32[3,4,32,128]{3,2,1,0:T(8,128)S(1)} collective-permute-done((f32[3,4,32,128]{3,2,1,0:T(8,128)S(1)}, f32[3,4,32,128]{3,2,1,0:T(8,128)S(1)}, u32[]{:S(2)}, u32[]{:S(2)}) %collective-permute-start.5) | collective-permute-done | bytes 196640 | tf_op jit(solution)/shard_map/ppermute | solution.py:528
  49.8 1.6 collective-permute-done.4
  51.5 0.4 collective-permute-start.6
  51.9 1.4 collective-permute-start.7
  53.3 0.2 pad_maximum_fusion
  53.5 4.4 %atmosphere.1 = f32[4,32,32,128]{3,2,1,0:T(8,128)} custom-call(f32[4,32,32,128]{3,2,1,0:T(8,128)} %state_ref.1, f32[32,128]{1,0:T(8,128)} %kappa_ref.1, f32[4,32,128]{2,1,0:T(8,128)} %bitcast.59), custom_call_target="tpu_custom_call" | custom-call | tf_op jit(solution)/shard_map/atmosphere/pallas_call | solution.py:146
  58.0 0.0 collective-permute-done.6
  58.0 0.0 collective-permute-done.7
  58.0 0.6 slice_multiply_fusion
  58.6 0.1 select_maximum_fusion.misc_ref
  58.7 103.1 %ocean.1 = f32[32,8,8,128]{3,2,1,0:T(8,128)S(1)} custom-call(f32[32,20,8,128]{3,2,1,0:T(8,128)S(1)} %bitcast.44, f32[32,8,128]{2,1,0:T(8,128)S(1)} %select_maximum_fusion.misc_ref), custom_call_target="tpu_custom_call" | custom-call | tf_op jit(solution)/shard_map/ocean/pallas_call | solution.py:494
  161.8 1.6 copy.25
  (17 shorter events, 0.2 us)
Async XLA Ops:
  0.6 45.7 %copy-start.2 = (f32[32,32,128]{2,1,0:T(8,128)S(1)}, f32[32,32,128]{2,1,0:T(8,128)}, u32[]{:S(2)}) copy-start(f32[32,32,128]{2,1,0:T(8,128)} %param.13) | copy-start | bytes 1572868
  1.5 8.7 %collective-permute-start.1 = (f32[1,96,128]{2,1,0:T(8,128)S(1)}, f32[1,96,128]{2,1,0:T(8,128)S(1)}, u32[]{:S(2)}, u32[]{:S(2)}) collective-permute-start(f32[1,96,128]{2,1,0:T(8,128)S(1)} %maximum_bitcast_fusion), channel_id=1, source_target_pairs={{1,0},{2,1},{3,2},{16,3},{17,16},{18,17},{19,18},{5,4},{6,5},{7,6}... | collective-permute-start | bytes 147464 | tf_op jit(solution)/shard_map/ppermute | solution.py:528
  3.8 7.9 %collective-permute-start = (f32[1,96,128]{2,1,0:T(8,128)S(1)}, f32[1,96,128]{2,1,0:T(8,128)S(1)}, u32[]{:S(2)}, u32[]{:S(2)}) collective-permute-start(f32[1,96,128]{2,1,0:T(8,128)S(1)} %maximum_bitcast_fusion), channel_id=1, source_target_pairs={{0,1},{1,2},{2,3},{3,16},{16,17},{17,18},{18,19},{4,5},{5,6},{6,7}... | collective-permute-start | bytes 147464 | tf_op jit(solution)/shard_map/ppermute | solution.py:528
  11.8 34.9 %copy-start = (f32[2,32,32,128]{3,2,1,0:T(8,128)S(1)}, f32[2,32,32,128]{3,2,1,0:T(8,128)}, u32[]{:S(2)}) copy-start(f32[2,32,32,128]{3,2,1,0:T(8,128)} %param.12) | copy-start | bytes 3145732
  11.8 6.6 %collective-permute-start.3 = (f32[3,96,128]{2,1,0:T(8,128)S(1)}, f32[3,96,128]{2,1,0:T(8,128)S(1)}, u32[]{:S(2)}, u32[]{:S(2)}) collective-permute-start(f32[3,96,128]{2,1,0:T(8,128)S(1)} %get-tuple-element.15), channel_id=1, source_target_pairs={{0,12},{4,0},{8,4},{12,8},{1,13},{5,1},{9,5},{13,9},{2,14},{6,2},{... | collective-permute-start | bytes 442376 | tf_op jit(solution)/shard_map/ppermute | solution.py:528
  11.9 6.5 %collective-permute-start.2 = (f32[3,96,128]{2,1,0:T(8,128)S(1)}, f32[3,96,128]{2,1,0:T(8,128)S(1)}, u32[]{:S(2)}, u32[]{:S(2)}) collective-permute-start(f32[3,96,128]{2,1,0:T(8,128)S(1)} %get-tuple-element.15), channel_id=1, source_target_pairs={{0,4},{4,8},{8,12},{12,0},{1,5},{5,9},{9,13},{13,1},{2,6},{6,10},{... | collective-permute-start | bytes 442376 | tf_op jit(solution)/shard_map/ppermute | solution.py:528
  19.2 28.1 %copy-start.1 = (f32[2,32,32,128]{3,2,1,0:T(8,128)S(1)}, f32[2,32,32,128]{3,2,1,0:T(8,128)}, u32[]{:S(2)}) copy-start(f32[2,32,32,128]{3,2,1,0:T(8,128)} %param.11) | copy-start | bytes 3145732
  37.5 12.3 %collective-permute-start.5 = (f32[3,4,32,128]{3,2,1,0:T(8,128)S(1)}, f32[3,4,32,128]{3,2,1,0:T(8,128)S(1)}, u32[]{:S(2)}, u32[]{:S(2)}) collective-permute-start(f32[3,4,32,128]{3,2,1,0:T(8,128)S(1)} %bitcast.54), channel_id=1, source_target_pairs={{1,0},{2,1},{3,2},{16,3},{17,16},{18,17},{19,18},{5,4},{6,5},{7,6}... | collective-permute-start | bytes 589832 | tf_op jit(solution)/shard_map/ppermute | solution.py:528
  39.4 12.0 %collective-permute-start.4 = (f32[3,4,32,128]{3,2,1,0:T(8,128)S(1)}, f32[3,4,32,128]{3,2,1,0:T(8,128)S(1)}, u32[]{:S(2)}, u32[]{:S(2)}) collective-permute-start(f32[3,4,32,128]{3,2,1,0:T(8,128)S(1)} %bitcast.53), channel_id=1, source_target_pairs={{0,1},{1,2},{2,3},{3,16},{16,17},{17,18},{18,19},{4,5},{5,6},{6,7}... | collective-permute-start | bytes 589832 | tf_op jit(solution)/shard_map/ppermute | solution.py:528
  51.5 6.5 %collective-permute-start.6 = (f32[4,32,128]{2,1,0:T(8,128)S(1)}, f32[4,32,128]{2,1,0:T(8,128)S(1)}, u32[]{:S(2)}, u32[]{:S(2)}) collective-permute-start(f32[4,32,128]{2,1,0:T(8,128)S(1)} %get-tuple-element.12), channel_id=1, source_target_pairs={{0,4},{4,8},{8,12},{12,0},{1,5},{5,9},{9,13},{13,1},{2,6},{6,10},{... | collective-permute-start | bytes 196616 | tf_op jit(solution)/shard_map/ppermute | solution.py:528
  51.9 1.7 %copy-start.3 = (s32[32,128]{1,0:T(8,128)S(1)}, s32[32,128]{1,0:T(8,128)}, u32[]{:S(2)}) copy-start(s32[32,128]{1,0:T(8,128)} %param.14) | copy-start | bytes 49156
  51.9 6.1 %collective-permute-start.7 = (f32[4,32,128]{2,1,0:T(8,128)S(1)}, f32[4,32,128]{2,1,0:T(8,128)S(1)}, u32[]{:S(2)}, u32[]{:S(2)}) collective-permute-start(f32[4,32,128]{2,1,0:T(8,128)S(1)} %get-tuple-element.13), channel_id=1, source_target_pairs={{0,12},{4,0},{8,4},{12,8},{1,13},{5,1},{9,5},{13,9},{2,14},{6,2},{... | collective-permute-start | bytes 196616 | tf_op jit(solution)/shard_map/ppermute | solution.py:528

commit v3 on v2

--- a/solution.py
+++ b/solution.py
@@ -170,9 +170,9 @@
 
 
 def ocean_kernel(
-    all_ref, misc_ref, st,
+    all_ref, misc_ref, edge_ref, st,
     halo0, halo_m, halo1, send0, recv0, send1, recv1, xt0, ping, pong, coef, force,
-    row0_send, row0_recv, misc_send, misc_recv, col0_send, col0_recv,
+    misc_send, misc_recv, col0_send, col0_recv,
     row_send, row_recv, col_send, col_recv,
     *, face_count, gy_count, gx_count,
 ):
@@ -209,7 +209,6 @@
     @pl.when(pos == 0)
     def _():
         def clear(r, _):
-            halo0[0, r] = jnp.zeros((groups, sub, cols), F32)
             halo_m[0, r] = jnp.zeros((sub, cols), F32)
             for e in range(rounds - 1):
                 for c in range(chunks):
@@ -252,8 +251,6 @@
 
     lane = lax.broadcasted_iota(jnp.int32, (sub, cols), 1)
     slot = lane // depth
-    first = lane == 0
-    final = lane == cols - 1
 
     def packed(value_of):
         to_east, to_west = None, None
@@ -272,17 +269,18 @@
         high = pltpu.roll(from_w, shift_w, 1) if shift_w else from_w
         return jnp.where(slot == 0, low, jnp.where(slot == per - 1, high, 0.0))
 
-    rows0 = row_copies(
-        all_ref.at[pl.ds(rows - depth, depth)], all_ref.at[pl.ds(0, depth)],
-        lambda s: halo0.at[s], lambda s: row0_send.at[s], lambda s: row0_recv.at[s],
-    )
     rows_m = row_copies(
         misc_ref.at[pl.ds(rows - depth, depth)], misc_ref.at[pl.ds(0, depth)],
         lambda s: halo_m.at[s], lambda s: misc_send.at[s], lambda s: misc_recv.at[s],
     )
-    begin(rows0)
     begin(rows_m)
-    finish(rows0)
+
+    def take(r, _):
+        halo0[0, r] = edge_ref[0, r]
+        halo0[1, r] = edge_ref[1, r]
+        return 0
+
+    lax.fori_loop(0, depth, take, 0)
     finish(rows_m)
 
     @pl.when(top)
@@ -418,28 +416,30 @@
             for r in range(tall):
                 ping[0, r, t] = row1(e, c, r, t)
 
+    lane2 = lax.broadcasted_iota(jnp.int32, (2, sub, cols), 2)
+    first2 = lane2 == 0
+    final2 = lane2 == cols - 1
+
     def steps(c):
         for s in range(depth):
             src, dst = (ping, pong) if s % 2 == 0 else (pong, ping)
             done = s == depth - 1
             for r in range(s + 1, tall - 1 - s):
-                for t in range(2):
-                    centre, extra = src[0, r, t], src[1, r, t]
-                    rc, rx = pltpu.roll(centre, 1, 1), pltpu.roll(extra, 1, 1)
-                    lc, lx = pltpu.roll(centre, cols - 1, 1), pltpu.roll(extra, cols - 1, 1)
-                    tiles = (
-                        (centre, jnp.where(first, rx, rc), jnp.where(final, lx, lc)),
-                        (extra, jnp.where(first, rc, rx), jnp.where(final, lc, lx)),
-                    )
-                    for i, (mine, w, e) in enumerate(tiles[:1] if done else tiles):
-                        new = coef[c, i, r, 0] * mine + (coef[c, i, r, 1] * w + coef[c, i, r, 2] * e)
-                        new = new + (
-                            coef[c, i, r, 3] * src[i, r - 1, t] + coef[c, i, r, 4] * src[i, r + 1, t]
-                        )
-                        if done:
-                            st[r - depth, 2 * c + t] = new
-                        else:
-                            dst[i, r, t] = new
+                centre, extra = src[0, r], src[1, r]
+                rc, rx = pltpu.roll(centre, 1, 2), pltpu.roll(extra, 1, 2)
+                lc, lx = pltpu.roll(centre, cols - 1, 2), pltpu.roll(extra, cols - 1, 2)
+                tiles = (
+                    (centre, jnp.where(first2, rx, rc), jnp.where(final2, lx, lc)),
+                    (extra, jnp.where(first2, rc, rx), jnp.where(final2, lc, lx)),
+                )
+                for i, (mine, w, e) in enumerate(tiles[:1] if done else tiles):
+                    k = coef[c, i, r]
+                    new = k[0:1] * mine + (k[1:2] * w + k[2:3] * e)
+                    new = new + (k[3:4] * src[i, r - 1] + k[4:5] * src[i, r + 1])
+                    if done:
+                        st[r - depth, pl.ds(2 * c, 2)] = new
+                    else:
+                        dst[i, r] = new
 
             @pl.when(c == 0)
             def _():
@@ -482,7 +482,7 @@
     lax.fori_loop(0, rounds * chunks, item, 0)
 
 
-def ocean(fields, misc):
+def ocean(fields, misc, edges):
     rows, groups, sub, cols = fields.shape
     chunks = groups // 5
     depth = DEPTH
@@ -496,7 +496,7 @@
             ocean_kernel, face_count=lax.axis_size("face"),
             gy_count=lax.axis_size("gy"), gx_count=lax.axis_size("gx"),
         ),
-        in_specs=[pl.BlockSpec(memory_space=pltpu.VMEM)] * 2,
+        in_specs=[pl.BlockSpec(memory_space=pltpu.VMEM)] * 3,
         out_specs=pl.BlockSpec(memory_space=pltpu.VMEM),
         out_shape=jax.ShapeDtypeStruct((rows, 2 * chunks, sub, cols), F32),
         scratch_shapes=[
@@ -512,14 +512,14 @@
             vm(2, tall, 2),
             vm(chunks, 2, tall, 5),
             vm(2, 2, tall),
-            dma(2), dma(2), dma(2), dma(2), dma(2), dma(2),
+            dma(2), dma(2), dma(2), dma(2),
             dma(later, chunks, 2), dma(later, chunks, 2), dma(later, chunks, 2), dma(later, chunks, 2),
         ],
         compiler_params=pltpu.CompilerParams(
             collective_id=0, has_side_effects=True, vmem_limit_bytes=48 * 1024 * 1024
         ),
         name="ocean",
-    )(fields, misc)
+    )(fields, misc, edges)
 
 
 def shifted(value, axis, step, wrap):
@@ -564,11 +564,17 @@
     fields = jnp.concatenate([ocean_tracers, ocean_flow, ocean_kappa[None]])
     fields = fields.reshape(5, levels // 8, 8, rows, cols).transpose(3, 1, 0, 2, 4)
     fields = fields.reshape(rows, 5 * levels // 8, 8, cols)
+    upper, lower = fields[rows - DEPTH :], fields[:DEPTH]
+    faces, lon, span = lax.axis_size("face"), lax.axis_size("gx"), lax.axis_size("gy")
+    tops = [((faces - 1) * lon + x) * span + span - 1 for x in range(lon)]
+    beyond = lax.ppermute(upper, ("face", "gx", "gy"), list(zip(tops, tops[::-1])))
+    beyond = beyond + shifted(lower, lat, -1, False)
+    edges = jnp.stack([shifted(upper, lat, 1, False), beyond])
     forcing = jnp.stack(
         [-ocean_gain * (ocean_flux[0] + ocean_flux[1]), ocean_gain * ocean_flux[1], sea_weight], axis=1
     )
     misc = jnp.pad(forcing, ((0, 0), (0, 5), (0, 0)))
-    ocean_now = ocean(fields, misc).reshape(rows, levels // 8, 2, 8, cols)
+    ocean_now = ocean(fields, misc, edges).reshape(rows, levels // 8, 2, 8, cols)
     ocean_now = ocean_now.transpose(2, 1, 3, 0, 4).reshape(ocean_tracers.shape)
     return (atmos_now, ocean_now, sea_weight * ocean_flux[2:4])
 

time: 164 us -> 169 us (1.030)
  Pallas kernels: 125 us -> 92.7 us
  waiting for transfers between devices: 5.21 us -> 29.8 us
  starting transfers between devices: 19.8 us -> 24.4 us
  local copies, waits for them, and re-layouts: 11.1 us -> 14.3 us
  other arithmetic: 1.86 us -> 4.94 us
    pallas_call x1, Pallas kernels: 103 us -> 71.2 us  [ocean(): pl.pallas_call(functools.partial(ocean_kernel, face_count=lax.axis_size('...]
    ppermute x8 -> x10, waiting for transfers between devices: 5.21 us -> 29.8 us  [shifted(): return lax.ppermute(value, axis, pairs)]
    unnamed x8, local copies, waits for them, and re-layouts: 0.02 us -> 3.75 us
    ppermute x8 -> x10, starting transfers between devices: 19.8 us -> 22.9 us  [shifted(): return lax.ppermute(value, axis, pairs)]
    another operation x0 -> x2, other arithmetic: none -> 2.53 us  [local(): edges = jnp.stack([shifted(upper, lat, 1, False), beyond])]
  transfers between devices with their start and end apart: 8 -> 11, of which waited for: 4 -> 5; matrix products, arithmetic and copies ran while one was open for 5% -> 8% of each run, Pallas kernels for 3% -> 3%
where the time goes in v3:
time: 169 us; the launch traced here: 167 us
  Pallas kernels  92.7 us (55%)
  waiting for transfers between devices  29.8 us (18%)
  starting transfers between devices  24.4 us (14%)
  local copies, waits for them, and re-layouts  14.3 us (8%)
  other arithmetic  4.94 us (3%)
    pallas_call x1, Pallas kernels, ocean(): pl.pallas_call(functools.partial(ocean_kernel, face_count=lax.axis_size('...  71.2 us
    ppermute x10, waiting for transfers between devices, shifted(): return lax.ppermute(value, axis, pairs)  29.8 us
    ppermute x10, starting transfers between devices, shifted(): return lax.ppermute(value, axis, pairs)  22.9 us
    pallas_call x1, Pallas kernels, xgrid(): pl.pallas_call(functools.partial(xgrid_kernel, rows=rows, cols=cols), gri...  17.1 us
    pallas_call x1, Pallas kernels, atmosphere(): pl.pallas_call(atmos_kernel, grid=(fields,), in_specs=[pl.BlockSpec((1, l...  4.42 us
    unnamed x8, local copies, waits for them, and re-layouts  3.75 us
  transfers between devices with their start and end apart: 11, of which 5 were waited for; matrix products, arithmetic and copies ran while one was open for 8% of the time, Pallas kernels for 3%

profile of v3, /device:TPU:24, one launch (start us, length us, event | category | flops | bytes accessed | tf_op | source)
XLA Modules:
  0.0 166.9 jit_solution(17817087969952421203)
XLA Ops:
  0.6 0.8 multiply_bitcast_fusion.1
  1.4 3.1 %collective-permute-start = (f32[1,96,128]{2,1,0:T(8,128)S(1)}, f32[1,96,128]{2,1,0:T(8,128)S(1)}, u32[]{:S(2)}, u32[]{:S(2)}) collective-permute-start(f32[1,96,128]{2,1,0:T(8,128)S(1)} %maximum_bitcast_fusion), channel_id=1, source_target_pairs={{0,1},{1,2},{2,3},{3,16},{16,17},{17,18},{18,19},{4,5},{5,6},{6,7}... | collective-permute-start | bytes 147464 | tf_op jit(solution)/shard_map/ppermute | solution.py:528
  4.5 2.8 %collective-permute-start.1 = (f32[1,96,128]{2,1,0:T(8,128)S(1)}, f32[1,96,128]{2,1,0:T(8,128)S(1)}, u32[]{:S(2)}, u32[]{:S(2)}) collective-permute-start(f32[1,96,128]{2,1,0:T(8,128)S(1)} %maximum_bitcast_fusion), channel_id=1, source_target_pairs={{1,0},{2,1},{3,2},{16,3},{17,16},{18,17},{19,18},{5,4},{6,5},{7,6}... | collective-permute-start | bytes 147464 | tf_op jit(solution)/shard_map/ppermute | solution.py:528
  7.3 1.8 %copy_dynamic-update-slice_fusion.1 = f32[5,4,8,32,128]{4,2,0,1,3:T(8,128)S(1)} fusion(f32[2,4,8,32,128]{4,3,2,1,0:T(8,128)} %bitcast.54), kind=kLoop, calls=%fused_computation.2 | loop fusion | bytes 2097152
  9.1 1.6 copy.20.w_ref
  10.7 1.5 slice.55
  12.2 1.5 reshape.85.acell_ref
  13.6 0.7 reshape.86.ocell_ref
  14.4 1.7 %collective-permute-start.3 = (f32[3,96,128]{2,1,0:T(8,128)S(1)}, f32[3,96,128]{2,1,0:T(8,128)S(1)}, u32[]{:S(2)}, u32[]{:S(2)}) collective-permute-start(f32[3,96,128]{2,1,0:T(8,128)S(1)} %get-tuple-element.17), channel_id=1, source_target_pairs={{0,12},{4,0},{8,4},{12,8},{1,13},{5,1},{9,5},{13,9},{2,14},{6,2},{... | collective-permute-start | bytes 442376 | tf_op jit(solution)/shard_map/ppermute | solution.py:528
  16.1 1.9 %copy_dynamic-update-slice_fusion = f32[5,4,8,32,128]{4,2,0,1,3:T(8,128)S(1)} fusion(f32[5,4,8,32,128]{4,2,0,1,3:T(8,128)S(1)} %copy_dynamic-update-slice_fusion.1, f32[2,4,8,32,128]{4,3,2,1,0:T(8,128)} %bitcast.53), kind=kLoop, calls=%fused_computation.1 | loop fusion | bytes 2097152
  18.0 0.9 collective-permute-done.2
  19.6 0.8 copy.19
  20.4 17.1 %xgrid.1 = (f32[128,128]{1,0:T(8,128)}, f32[9,128,128]{2,1,0:T(8,128)}) custom-call(f32[128,128]{1,0:T(8,128)} %bitcast.60, f32[9,96,128]{2,1,0:T(8,128)} %bitcast.52, s32[9,1,1024]{2,1,0:T(1,128)} %reshape.85.acell_ref, s32[9,1,1024]{2,1,0:T(1,128)} %reshape.86.ocell_ref, f32[2,9,1,1024]{3,2,1,0:T(1,128)} %copy.20.w_ref), custom_call_target="tpu_custom_call" | custom-call | tf_op jit(solution)/shard_map/xgrid/pallas_call | solution.py:105
  37.4 1.2 fusion.5
  38.6 5.8 %collective-permute-start.4 = (f32[3,4,32,128]{3,2,1,0:T(8,128)S(1)}, f32[3,4,32,128]{3,2,1,0:T(8,128)S(1)}, u32[]{:S(2)}, u32[]{:S(2)}) collective-permute-start(f32[3,4,32,128]{3,2,1,0:T(8,128)S(1)} %bitcast.62), channel_id=1, source_target_pairs={{0,1},{1,2},{2,3},{3,16},{16,17},{17,18},{18,19},{4,5},{5,6},{6,7}... | collective-permute-start | bytes 589832 | tf_op jit(solution)/shard_map/ppermute | solution.py:528
  44.4 1.9 %collective-permute-start.5 = (f32[3,4,32,128]{3,2,1,0:T(8,128)S(1)}, f32[3,4,32,128]{3,2,1,0:T(8,128)S(1)}, u32[]{:S(2)}, u32[]{:S(2)}) collective-permute-start(f32[3,4,32,128]{3,2,1,0:T(8,128)S(1)} %bitcast.61), channel_id=1, source_target_pairs={{1,0},{2,1},{3,2},{16,3},{17,16},{18,17},{19,18},{5,4},{6,5},{7,6}... | collective-permute-start | bytes 589832 | tf_op jit(solution)/shard_map/ppermute | solution.py:528
  46.6 3.0 %collective-permute-done.4 = f32[3,4,32,128]{3,2,1,0:T(8,128)S(1)} collective-permute-done((f32[3,4,32,128]{3,2,1,0:T(8,128)S(1)}, f32[3,4,32,128]{3,2,1,0:T(8,128)S(1)}, u32[]{:S(2)}, u32[]{:S(2)}) %collective-permute-start.4) | collective-permute-done | bytes 196640 | tf_op jit(solution)/shard_map/ppermute | solution.py:528
  49.6 6.9 %collective-permute-done.5 = f32[3,4,32,128]{3,2,1,0:T(8,128)S(1)} collective-permute-done((f32[3,4,32,128]{3,2,1,0:T(8,128)S(1)}, f32[3,4,32,128]{3,2,1,0:T(8,128)S(1)}, u32[]{:S(2)}, u32[]{:S(2)}) %collective-permute-start.5) | collective-permute-done | bytes 196640 | tf_op jit(solution)/shard_map/ppermute | solution.py:528
  56.5 0.7 slice_bitcast_fusion.1
  57.2 1.7 %collective-permute-start.7 = (f32[4,32,128]{2,1,0:T(8,128)}, f32[4,32,128]{2,1,0:T(8,128)}, u32[]{:S(2)}, u32[]{:S(2)}) collective-permute-start(f32[4,32,128]{2,1,0:T(8,128)} %get-tuple-element.15), channel_id=1, source_target_pairs={{0,12},{4,0},{8,4},{12,8},{1,13},{5,1},{9,5},{13,9},{2,14},{6,2},{... | collective-permute-start | bytes 196616 | tf_op jit(solution)/shard_map/ppermute | solution.py:528
  59.0 0.9 fusion.4
  59.9 1.5 collective-permute-start.9
  61.4 1.9 %collective-permute-start.8 = (f32[8,20,8,128]{3,2,1,0:T(8,128)S(1)}, f32[8,20,8,128]{3,2,1,0:T(8,128)}, u32[]{:S(2)}, u32[]{:S(2)}) collective-permute-start(f32[8,20,8,128]{3,2,1,0:T(8,128)S(1)} %bitcast.58), channel_id=1, source_target_pairs={{0,1},{1,2},{2,3},{3,16},{16,17},{17,18},{18,19},{4,5},{5,6},{6,7}... | collective-permute-start | bytes 1966088 | tf_op jit(solution)/shard_map/ppermute | solution.py:528
  63.3 3.9 %collective-permute-start.10 = (f32[8,20,8,128]{3,2,1,0:T(8,128)}, f32[8,20,8,128]{3,2,1,0:T(8,128)}, u32[]{:S(2)}, u32[]{:S(2)}) collective-permute-start(f32[8,20,8,128]{3,2,1,0:T(8,128)} %bitcast.28), channel_id=1, source_target_pairs={{1,0},{2,1},{3,2},{16,3},{17,16},{18,17},{19,18},{5,4},{6,5},{7,6}... | collective-permute-start | bytes 1966088 | tf_op jit(solution)/shard_map/ppermute | solution.py:528
  67.3 4.4 %atmosphere.1 = f32[4,32,32,128]{3,2,1,0:T(8,128)} custom-call(f32[4,32,32,128]{3,2,1,0:T(8,128)} %state_ref.1, f32[32,128]{1,0:T(8,128)} %kappa_ref.1, f32[4,32,128]{2,1,0:T(8,128)} %bitcast.67), custom_call_target="tpu_custom_call" | custom-call | tf_op jit(solution)/shard_map/atmosphere/pallas_call | solution.py:146
  71.7 0.9 fusion.1
  72.6 0.6 slice_multiply_fusion
  73.3 18.4 %collective-permute-done.10 = f32[8,20,8,128]{3,2,1,0:T(8,128)} collective-permute-done((f32[8,20,8,128]{3,2,1,0:T(8,128)}, f32[8,20,8,128]{3,2,1,0:T(8,128)}, u32[]{:S(2)}, u32[]{:S(2)}) %collective-permute-start.10) | collective-permute-done | bytes 655392 | tf_op jit(solution)/shard_map/ppermute | solution.py:528
  91.6 1.4 add_bitcast_fusion
  93.0 1.2 pad_maximum_fusion.edge_ref
  94.2 71.2 %ocean.1 = f32[32,8,8,128]{3,2,1,0:T(8,128)S(1)} custom-call(f32[32,20,8,128]{3,2,1,0:T(8,128)S(1)} %bitcast.50, f32[32,8,128]{2,1,0:T(8,128)S(1)} %select_maximum_fusion.misc_ref, f32[2,8,20,8,128]{4,3,2,1,0:T(8,128)S(1)} %pad_maximum_fusion.edge_ref), custom_call_target="tpu_custom_call" | custom-call | tf_op jit(solution)/shard_map/ocean/pallas_call | solution.py:494
  165.4 1.6 copy.25
  (23 shorter events, 1.2 us)
Async XLA Ops:
  0.6 13.0 %copy-start.1 = (s32[3,3,1024]{2,1,0:T(4,128)S(1)}, s32[3,3,1024]{2,1,0:T(4,128)}, u32[]{:S(2)}) copy-start(s32[3,3,1024]{2,1,0:T(4,128)} %param.16) | copy-start | bytes 110596
  1.4 12.9 %collective-permute-start = (f32[1,96,128]{2,1,0:T(8,128)S(1)}, f32[1,96,128]{2,1,0:T(8,128)S(1)}, u32[]{:S(2)}, u32[]{:S(2)}) collective-permute-start(f32[1,96,128]{2,1,0:T(8,128)S(1)} %maximum_bitcast_fusion), channel_id=1, source_target_pairs={{0,1},{1,2},{2,3},{3,16},{16,17},{17,18},{18,19},{4,5},{5,6},{6,7}... | collective-permute-start | bytes 147464 | tf_op jit(solution)/shard_map/ppermute | solution.py:528
  4.5 9.8 %collective-permute-start.1 = (f32[1,96,128]{2,1,0:T(8,128)S(1)}, f32[1,96,128]{2,1,0:T(8,128)S(1)}, u32[]{:S(2)}, u32[]{:S(2)}) collective-permute-start(f32[1,96,128]{2,1,0:T(8,128)S(1)} %maximum_bitcast_fusion), channel_id=1, source_target_pairs={{1,0},{2,1},{3,2},{16,3},{17,16},{18,17},{19,18},{5,4},{6,5},{7,6}... | collective-permute-start | bytes 147464 | tf_op jit(solution)/shard_map/ppermute | solution.py:528
  14.3 4.6 %collective-permute-start.2 = (f32[3,96,128]{2,1,0:T(8,128)S(1)}, f32[3,96,128]{2,1,0:T(8,128)S(1)}, u32[]{:S(2)}, u32[]{:S(2)}) collective-permute-start(f32[3,96,128]{2,1,0:T(8,128)S(1)} %get-tuple-element.17), channel_id=1, source_target_pairs={{0,4},{4,8},{8,12},{12,0},{1,5},{5,9},{9,13},{13,1},{2,6},{6,10},{... | collective-permute-start | bytes 442376 | tf_op jit(solution)/shard_map/ppermute | solution.py:528
  14.4 5.2 %collective-permute-start.3 = (f32[3,96,128]{2,1,0:T(8,128)S(1)}, f32[3,96,128]{2,1,0:T(8,128)S(1)}, u32[]{:S(2)}, u32[]{:S(2)}) collective-permute-start(f32[3,96,128]{2,1,0:T(8,128)S(1)} %get-tuple-element.17), channel_id=1, source_target_pairs={{0,12},{4,0},{8,4},{12,8},{1,13},{5,1},{9,5},{13,9},{2,14},{6,2},{... | collective-permute-start | bytes 442376 | tf_op jit(solution)/shard_map/ppermute | solution.py:528
  16.1 30.2 %copy-start = (f32[32,32,128]{2,1,0:T(8,128)S(1)}, f32[32,32,128]{2,1,0:T(8,128)}, u32[]{:S(2)}) copy-start(f32[32,32,128]{2,1,0:T(8,128)} %param.13) | copy-start | bytes 1572868
  38.6 28.6 %copy-start.2 = (s32[32,128]{1,0:T(8,128)S(1)}, s32[32,128]{1,0:T(8,128)}, u32[]{:S(2)}) copy-start(s32[32,128]{1,0:T(8,128)} %param.14) | copy-start | bytes 49156
  38.6 11.0 %collective-permute-start.4 = (f32[3,4,32,128]{3,2,1,0:T(8,128)S(1)}, f32[3,4,32,128]{3,2,1,0:T(8,128)S(1)}, u32[]{:S(2)}, u32[]{:S(2)}) collective-permute-start(f32[3,4,32,128]{3,2,1,0:T(8,128)S(1)} %bitcast.62), channel_id=1, source_target_pairs={{0,1},{1,2},{2,3},{3,16},{16,17},{17,18},{18,19},{4,5},{5,6},{6,7}... | collective-permute-start | bytes 589832 | tf_op jit(solution)/shard_map/ppermute | solution.py:528
  44.4 12.1 %collective-permute-start.5 = (f32[3,4,32,128]{3,2,1,0:T(8,128)S(1)}, f32[3,4,32,128]{3,2,1,0:T(8,128)S(1)}, u32[]{:S(2)}, u32[]{:S(2)}) collective-permute-start(f32[3,4,32,128]{3,2,1,0:T(8,128)S(1)} %bitcast.61), channel_id=1, source_target_pairs={{1,0},{2,1},{3,2},{16,3},{17,16},{18,17},{19,18},{5,4},{6,5},{7,6}... | collective-permute-start | bytes 589832 | tf_op jit(solution)/shard_map/ppermute | solution.py:528
  57.2 14.5 %collective-permute-start.6 = (f32[4,32,128]{2,1,0:T(8,128)}, f32[4,32,128]{2,1,0:T(8,128)S(1)}, u32[]{:S(2)}, u32[]{:S(2)}) collective-permute-start(f32[4,32,128]{2,1,0:T(8,128)} %get-tuple-element.14), channel_id=1, source_target_pairs={{0,4},{4,8},{8,12},{12,0},{1,5},{5,9},{9,13},{13,1},{2,6},{6,10},{... | collective-permute-start | bytes 196616 | tf_op jit(solution)/shard_map/ppermute | solution.py:528
  57.2 14.5 %collective-permute-start.7 = (f32[4,32,128]{2,1,0:T(8,128)}, f32[4,32,128]{2,1,0:T(8,128)}, u32[]{:S(2)}, u32[]{:S(2)}) collective-permute-start(f32[4,32,128]{2,1,0:T(8,128)} %get-tuple-element.15), channel_id=1, source_target_pairs={{0,12},{4,0},{8,4},{12,8},{1,13},{5,1},{9,5},{13,9},{2,14},{6,2},{... | collective-permute-start | bytes 196616 | tf_op jit(solution)/shard_map/ppermute | solution.py:528
  59.9 13.4 %collective-permute-start.9 = (f32[8,20,8,128]{3,2,1,0:T(8,128)S(1)}, f32[8,20,8,128]{3,2,1,0:T(8,128)}, u32[]{:S(2)}, u32[]{:S(2)}) collective-permute-start(f32[8,20,8,128]{3,2,1,0:T(8,128)S(1)} %bitcast.57), channel_id=1, source_target_pairs={{19,31},{23,27},{27,23},{31,19}} | collective-permute-start | bytes 1966088 | tf_op jit(solution)/shard_map/ppermute | solution.py:570
  61.4 31.6 %collective-permute-start.8 = (f32[8,20,8,128]{3,2,1,0:T(8,128)S(1)}, f32[8,20,8,128]{3,2,1,0:T(8,128)}, u32[]{:S(2)}, u32[]{:S(2)}) collective-permute-start(f32[8,20,8,128]{3,2,1,0:T(8,128)S(1)} %bitcast.58), channel_id=1, source_target_pairs={{0,1},{1,2},{2,3},{3,16},{16,17},{17,18},{18,19},{4,5},{5,6},{6,7}... | collective-permute-start | bytes 1966088 | tf_op jit(solution)/shard_map/ppermute | solution.py:528
  63.3 28.3 %collective-permute-start.10 = (f32[8,20,8,128]{3,2,1,0:T(8,128)}, f32[8,20,8,128]{3,2,1,0:T(8,128)}, u32[]{:S(2)}, u32[]{:S(2)}) collective-permute-start(f32[8,20,8,128]{3,2,1,0:T(8,128)} %bitcast.28), channel_id=1, source_target_pairs={{1,0},{2,1},{3,2},{16,3},{17,16},{18,17},{19,18},{5,4},{6,5},{7,6}... | collective-permute-start | bytes 1966088 | tf_op jit(solution)/shard_map/ppermute | solution.py:528
